TPU v7x, 256 devices: a whole 4x4x8 slice. The times are simulated.
256 devices in a mesh: leaf: 4 (over x), row: 8 (over z_lo, core), col: 8 (over z_hi, y).
Axes of the slice: x: 4, y: 4, z: 8 (z_hi: 2, z_lo: 4; z = z_hi * 4 + z_lo), core: 2. Of those that a mesh axis runs over, the one named last changes fastest.
Arguments:
- root_inverse: float32 [4096, 4096], P('row', ('leaf', 'col')), may hold values from -48 to 48, as said below
- lower_panel: float32 [4, 4096, 4096], P('leaf', 'row', 'col'), may hold values from -0.375 to 0.375
- panel_mask: int32 [4, 16, 16], P('leaf', 'row', 'col'), may hold values from 0 to 1, as said below
- factor_inverse: float32 [4, 4096, 4096], P('leaf', 'row', 'col'), may hold values from -8 to 8, as said below
Outputs:
- cross_inverse: float32 [4, 4096, 4096], P('leaf', 'row', 'col')
- block_inverse: float32 [4, 4096, 4096], P('leaf', 'row', 'col')
Inputs may be any that keep to these rules, and one draw needn't show every extreme that they name: `panel_mask`: each entry says whether the 256 x 256 block of a child's panel is kept; the share of kept blocks differs from block row to block row. `root_inverse`: symmetric and positive definite. `factor_inverse`: each child's matrix is symmetric and positive definite.
All inputs are finite; a program needn't handle non-finite values.
Results may differ from a plain program's by a relative error of at most 0.0001.
Values sent between devices are 32-bit elements; how exact they have to be, the bound alone decides.
No kernel may reach another device: no remote copies, remote signals or barrier semaphores. Data moves between devices by JAX's collectives and lax.ppermute only.
A program may use at most 192 MiB of HBM per device.

v0:
```python
import functools

import jax
import jax.numpy as jnp
from jax import lax
from jax.experimental import pallas as pl
from jax.experimental.pallas import tpu as pltpu
from jax.sharding import Mesh
from jax.sharding import PartitionSpec as P

AXES = ("leaf", "z_lo", "core", "z_hi", "y")
COL = ("z_hi", "y")
NX, NL, NH, NY = 4, 4, 2, 4
NZ = NL * NH
F32 = jnp.float32
HBM = pl.BlockSpec(memory_space=pltpu.HBM)
SMEM = pl.BlockSpec(memory_space=pltpu.SMEM)
VMEM = pl.BlockSpec(memory_space=pltpu.VMEM)
PARAMS = pltpu.CompilerParams(vmem_limit_bytes=56 << 20)
SMALL = pltpu.CompilerParams(vmem_limit_bytes=16 << 20)


def way(core):
    return 1 if core == 0 else -1


def z_step(block):
    def place(z, core):
        return ((z % NL) * 2 + core) * NH + z // NL

    pairs = [(place(z, core), place((z + way(core)) % NZ, core)) for z in range(NZ) for core in range(2)]
    return lax.ppermute(block, ("z_lo", "core", "z_hi"), pairs)


def y_step(block):
    pairs = [(core * NY + y, core * NY + (y + way(core)) % NY) for y in range(NY) for core in range(2)]
    return lax.ppermute(block, ("core", "y"), pairs)


def x_step(block):
    pairs = [(x * 2 + core, (x + way(core)) % NX * 2 + core) for x in range(NX) for core in range(2)]
    return lax.ppermute(block, ("leaf", "core"), pairs)


def swap(block, axis):
    return lax.ppermute(block, axis, [(0, 1), (1, 0)])


def swap_both(halves):
    return [swap(half, "core") for half in halves]


def split(value):
    high = value.astype(jnp.bfloat16)
    return high, (value - high.astype(F32)).astype(jnp.bfloat16)


def products(lefts, right):
    dot = functools.partial(jnp.dot, preferred_element_type=F32)
    right_high, right_low = split(right)
    outs = []
    for left in lefts:
        left_high, left_low = split(left)
        outs.append(dot(left_high, right_high) + (dot(left_high, right_low) + dot(left_low, right_high)))
    return outs


def cost(dots, n):
    return pl.CostEstimate(flops=6 * dots * n**3, bytes_accessed=12 * dots * n * n, transcendentals=0)


def light(n):
    return pl.CostEstimate(flops=n * n, bytes_accessed=12 * n * n, transcendentals=0)


def shaped(*shape):
    return jax.ShapeDtypeStruct(shape, F32)


class Place:
    def __init__(self, ref):
        self.x, self.zl, self.core, self.zh, self.y = (ref[i] for i in range(5))
        self.z = self.zh * NL + self.zl
        self.turn = 1 - 2 * self.core


def mask_kernel(mask, panel, out, turned):
    h = out.shape[0] // 2
    for i in range(2):
        for j in range(2):
            rows, cols = slice(i * h, (i + 1) * h), slice(j * h, (j + 1) * h)
            part = panel[0, rows, cols] * mask[0, i, j].astype(F32)
            out[rows, cols] = part
            turned[cols, rows] = part.T


def masked_block(mask, panel):
    n = panel.shape[1]
    return pl.pallas_call(
        mask_kernel,
        out_shape=(shaped(n, n), shaped(n, n)),
        in_specs=[SMEM, VMEM],
        out_specs=(VMEM, VMEM),
        compiler_params=SMALL,
        cost_estimate=light(n),
    )(mask, panel)


def turn_kernel(block, turned):
    turned[...] = block[...].T


def turned_block(block):
    n = block.shape[0]
    return pl.pallas_call(
        turn_kernel,
        out_shape=shaped(n, n),
        in_specs=[VMEM],
        out_specs=VMEM,
        compiler_params=SMALL,
        cost_estimate=light(n),
    )(block)


class Step:
    def __init__(self, here, have, had, c):
        self.arrival = have[0] - 1 - c // 2
        from_x = here.x - here.turn * self.arrival
        self.s = jnp.bitwise_and(here.turn * (here.z - from_x), NL - 1) + NL * lax.rem(c, 2)
        self.half = jnp.bitwise_and(here.z - here.turn * self.s, NZ - 1) // NL
        before = jnp.logical_and(self.arrival < had[0], self.s < had[1])
        self.ready = jnp.logical_and(self.s < have[1], jnp.logical_not(before))


class Gather:
    def __init__(self, here, have, had, roots, ring, buffers):
        self.here, self.have, self.had, self.roots, self.ring = here, have, had, roots, ring
        self.left_buffer, self.right_buffer, self.left_sems, self.right_sems = buffers

    def step(self, c):
        return Step(self.here, self.have, self.had, c)

    def start(self, c, slot):
        here, step = self.here, self.step(c)
        left, right = self.left_buffer, self.right_buffer

        @pl.when(step.ready)
        def _():
            for t, pieces in enumerate(self.roots):

                @pl.when(step.arrival == t)
                def _():
                    q = pieces[0].shape[3]
                    for p in range(NY):
                        at = pl.multiple_of(jnp.bitwise_and(here.y - p, NY - 1) * q, q)
                        source, to = pieces[p // 2].at[p % 2], left.at[slot, :, :, pl.ds(at, q)]
                        pltpu.make_async_copy(source, to, self.left_sems.at[slot]).start()

            for k, block in enumerate(self.ring):

                @pl.when(step.s == k)
                def _():
                    pltpu.make_async_copy(block, right.at[slot], self.right_sems.at[slot]).start()

    def run(self, totals):
        steps = 2 * self.have[0]

        @pl.loop(0, steps)
        def _(c):
            slot = lax.rem(c, 2)

            @pl.when(c + 1 < steps)
            def _():
                self.start(c + 1, 1 - slot)

            step = self.step(c)

            @pl.when(step.ready)
            def _():
                for buffer, sems in ((self.left_buffer, self.left_sems), (self.right_buffer, self.right_sems)):
                    pltpu.make_async_copy(buffer.at[slot], buffer.at[slot], sems.at[slot]).wait()
                left = self.left_buffer
                for total, out in zip(totals, products((left[slot, 0], left[slot, 1]), self.right_buffer[slot])):
                    total[step.half] = total[step.half] + out


class Pair:
    def __init__(self, here, left, buffer, sems):
        self.here, self.left, self.buffer, self.sems = here, left, buffer, sems

    def target(self, i):
        here = self.here
        own = lax.rem(i, 2)
        to_z = jnp.bitwise_and(here.z + here.turn * (2 * own - 1) * (i // 2), NZ - 1)
        return jnp.bitwise_and(to_z, NL - 1) * 2 + jnp.where(own == 1, here.core, 1 - here.core), to_z // NL

    def start(self, i):
        here = self.here
        block, _ = self.target(i)
        step = jnp.bitwise_and(here.turn * (here.y - jnp.bitwise_and(block, NY - 1)), NY - 1)
        index = jnp.where(block // NY == here.zh, step, step + NY)
        slot = lax.rem(i, 2)
        for k, ref in enumerate(self.left):

            @pl.when(index == k)
            def _():
                pltpu.make_async_copy(ref, self.buffer.at[slot], self.sems.at[slot]).start()

    def run(self, order, outs, total):
        first, last = 2 * order[0], 2 * order[-1]

        @pl.loop(0, 2 * len(order))
        def _(k):
            i = first - k // 2 * 2 + lax.rem(k, 2)
            slot = lax.rem(k, 2)
            pltpu.make_async_copy(self.buffer.at[slot], self.buffer.at[slot], self.sems.at[slot]).wait()
            (out,) = products((self.buffer[slot],), total[self.target(i)[1]])
            for j, (top, bottom) in enumerate(outs):
                h = top.shape[0]

                @pl.when(k == j)
                def _():
                    top[...] = out[:h]
                    bottom[...] = out[h:]

            @pl.when(i - 2 >= last)
            def _():
                self.start(i - 2)


def unpack(refs, sizes):
    parts = []
    for size in sizes:
        parts.append(refs[:size])
        refs = refs[size:]
    return parts + [refs]


def groups(refs, size):
    return [refs[i : i + size] for i in range(0, len(refs), size)]


def load(source, target, sem):
    copy = pltpu.make_async_copy(source, target, sem)
    copy.start()
    copy.wait()


def gather_kernel(have, had, place, *refs):
    roots, ring, before, afters, rest = unpack(refs, (2 * have[0], have[1], 2 if had[1] else 0, 2))
    left_buffer, right_buffer, own, theirs, left_sems, right_sems, sems = rest
    totals = (own, theirs)
    buffers = (left_buffer, right_buffer, left_sems, right_sems)
    gather = Gather(Place(place), have, had, groups(roots, 2), ring, buffers)
    gather.start(0, 0)
    loads = [pltpu.make_async_copy(ref, total, sems.at[k]) for k, (ref, total) in enumerate(zip(before, totals))]
    for copy in loads:
        copy.start()
    for copy in loads:
        copy.wait()
    if not loads:
        for total in totals:
            total[...] = jnp.zeros_like(total)
    gather.run(totals)
    stores = [pltpu.make_async_copy(total, ref, sems.at[k]) for k, (ref, total) in enumerate(zip(afters, totals))]
    for copy in stores:
        copy.start()
    for copy in stores:
        copy.wait()


def accumulate(place, have, had, roots, ring, totals):
    n = ring[0].shape[0]
    operands = [place] + [part for pieces in roots[: have[0]] for part in pieces]
    operands += ring[: have[1]]
    aliases = {}
    if had[1]:
        aliases = {len(operands): 0, len(operands) + 1: 1}
        operands += totals
    block = pltpu.VMEM((2, n, n), F32)
    pair = pltpu.SemaphoreType.DMA((2,))
    return pl.pallas_call(
        functools.partial(gather_kernel, have, had),
        out_shape=(shaped(2, n, n),) * 2,
        in_specs=[SMEM] + [HBM] * (len(operands) - 1),
        out_specs=(HBM,) * 2,
        scratch_shapes=[pltpu.VMEM((2, 2, n, n), F32), block, block, block, pair, pair, pair],
        input_output_aliases=aliases,
        compiler_params=PARAMS,
        cost_estimate=cost(6, n),
    )(*operands)


def first_kernel(order, place, *refs):
    left, (own, theirs, ancestor), outs, (buffer, total, extra, sems, total_sems) = unpack(refs, (2 * NY, 3, 4 * len(order)))
    pair = Pair(Place(place), left, buffer, sems)
    pair.start(2 * order[0])
    pair.start(2 * order[0] + 1)
    loads = [pltpu.make_async_copy(a, b, total_sems.at[k]) for k, (a, b) in enumerate(((own, total), (theirs, extra)))]
    for copy in loads:
        copy.start()
    for copy in loads:
        copy.wait()
    total[...] = total[...] + extra[...]
    store = pltpu.make_async_copy(total, ancestor, total_sems.at[0])
    store.start()
    pair.run(order, groups(outs, 2), total)
    store.wait()


def first_pairs(place, order, left, own, theirs):
    n = left[0].shape[0]
    block = pltpu.VMEM((2, n, n), F32)
    pair = pltpu.SemaphoreType.DMA((2,))

    def body(place, *refs):
        ins, outs = refs[: len(left) + 2], refs[len(left) + 2 :]
        first_kernel(order, place, *ins, *outs)

    return pl.pallas_call(
        body,
        out_shape=(shaped(2, n, n),) + (shaped(n // 2, n),) * (4 * len(order)),
        in_specs=[SMEM] + [HBM] * (len(left) + 2),
        out_specs=(HBM,) + (VMEM,) * (4 * len(order)),
        scratch_shapes=[block, block, block, pair, pair],
        compiler_params=PARAMS,
        cost_estimate=cost(2, n),
    )(place, *left, own, theirs)


def pair_kernel(order, place, *refs):
    left, (right,), outs, (buffer, total, sems, sem) = unpack(refs, (2 * NY, 1, 4 * len(order)))
    pair = Pair(Place(place), left, buffer, sems)
    pair.start(2 * order[0])
    pair.start(2 * order[0] + 1)
    load(right, total, sem)
    pair.run(order, groups(outs, 2), total)


def pairs(place, order, left, right, dots):
    n = left[0].shape[0]
    block = pltpu.VMEM((2, n, n), F32)
    outs = pl.pallas_call(
        functools.partial(pair_kernel, order),
        out_shape=(shaped(n // 2, n),) * (4 * len(order)),
        in_specs=[SMEM] + [HBM] * (len(left) + 1),
        out_specs=(VMEM,) * (4 * len(order)),
        scratch_shapes=[block, block, pltpu.SemaphoreType.DMA((2,)), pltpu.SemaphoreType.DMA],
        compiler_params=PARAMS,
        cost_estimate=cost(dots, n),
    )(place, *left, right)
    return groups(outs, 4)


def cross_kernel(place, mask, total, out, buffer, sem):
    here = Place(place)
    copy = pltpu.make_async_copy(total.at[here.zh], buffer, sem)
    copy.start()
    copy.wait()
    h = buffer.shape[0] // 2
    for i in range(2):
        for j in range(2):
            rows, cols = slice(i * h, (i + 1) * h), slice(j * h, (j + 1) * h)
            out[0, rows, cols] = -(buffer[rows, cols] * mask[0, i, j].astype(F32))


def cross_block(place, mask, total):
    n = total.shape[1]
    return pl.pallas_call(
        cross_kernel,
        out_shape=shaped(1, n, n),
        in_specs=[SMEM, SMEM, HBM],
        out_specs=VMEM,
        scratch_shapes=[pltpu.VMEM((n, n), F32), pltpu.SemaphoreType.DMA],
        compiler_params=SMALL,
        cost_estimate=light(n),
    )(place, mask, total)


def from_all_y(part):
    return [part] + [lax.ppermute(part, "y", [(y, (y + k) % NY) for y in range(NY)]) for k in range(1, NY)]


def per_device(root_inverse, lower_panel, panel_mask, factor_inverse):
    place = jnp.stack([lax.axis_index(name) for name in AXES]).astype(jnp.int32)
    core, zh = lax.axis_index("core"), lax.axis_index("z_hi")
    away = swap(root_inverse, "z_hi")
    mine, turned = masked_block(panel_mask, lower_panel)

    good = core == zh
    kept, sent = jnp.where(good, root_inverse, away), jnp.where(good, away, root_inverse)
    piece, mine, turned = lax.optimization_barrier((jnp.stack([kept, swap(sent, "core")]), mine, turned))

    ring, rows_near, rows_far = [mine], [turned], []
    had, totals = (0, 0), ()
    for r in range(NX):
        ends = [ring]
        ring.append(z_step(ring[-1]))
        if r == 0:
            pieces = from_all_y(piece)
            ring[1], pieces[1], pieces[3] = lax.optimization_barrier((ring[1], pieces[1], pieces[3]))
        if len(ring) < NZ:
            ring.append(z_step(ring[-1]))
        if r == 0:
            groups_of = [[jnp.stack(pieces[:2])], [jnp.stack(pieces[2:])]]
        else:
            for group in groups_of:
                group.append(x_step(group[-1]))
            for _ in range(2):
                rows = rows_near if len(rows_near) < NY else rows_far
                rows.append(y_step(rows[-1]))
            ends += [rows_near] if r == 1 else [rows_near, rows_far] if r == 2 else [rows_far]
        ends += groups_of
        values = [into[-1] for into in ends]
        if r == NX - 1:
            had = (NX - 1, NZ - 1)
            totals = accumulate(place, had, (0, 0), list(zip(*groups_of)), ring, totals)
            totals, values = lax.optimization_barrier((totals, values))
        else:
            values = lax.optimization_barrier(values)
        for into, value in zip(ends, values):
            into[-1] = value
        if r == 1:
            rows_far = [turned_block(ring[NL])]
    roots = list(zip(*groups_of))
    own, theirs = accumulate(place, (NX, NZ), had, roots, ring, totals)

    rows = rows_near + rows_far
    total, *outs = first_pairs(place, [NL - 1, NL - 2], rows, own, swap(theirs, "core"))
    cross = cross_block(place, panel_mask, total)
    out, *outs = groups(outs, 4)
    moving = [own + theirs for own, theirs in zip(out[2:], swap_both(out[:2]))]
    moving, total = lax.optimization_barrier((moving, total))
    moving = [z_step(half) for half in moving]
    outs += pairs(place, list(range(NL - 3, -1, -1)), rows, total, 0)
    for out in outs[:-1]:
        moving = [z_step(a + own + theirs) for a, own, theirs in zip(moving, out[2:], swap_both(out[:2]))]
    out = outs[-1]
    rest = [a + own + theirs for a, own, theirs in zip(moving, out[2:], swap_both(out[:2]))]
    return cross, factor_inverse + jnp.concatenate(rest, 0)[None]


def solution(mesh):
    split_mesh = Mesh(mesh.devices.reshape(NX, NL, 2, NH, NY), AXES)
    row = ("z_lo", "core")
    block = P("leaf", row, COL)
    return jax.shard_map(
        per_device,
        mesh=split_mesh,
        in_specs=(P(row, ("leaf",) + COL), block, block, block),
        out_specs=(block, block),
        check_vma=False,
    )
```

profile of v0, /device:TPU:10, one launch (start us, length us, event | category | flops | bytes accessed | tf_op | source)
XLA Modules:
  0.0 235.5 jit_solution(16883495421724543195)
XLA Ops:
  0.6 7.3 %collective-permute-start = (f32[512,128]{1,0:T(8,128)}, f32[512,128]{1,0:T(8,128)S(1)}, u32[]{:S(2)}, u32[]{:S(2)}) collective-permute-start(f32[512,128]{1,0:T(8,128)} %param.4), channel_id=1, source_target_pairs={{0,4},{4,0},{1,5},{5,1},{2,6},{6,2},{3,7},{7,3},{8,12},{12,8},{9,1... | collective-permute-start | bytes 786440 | tf_op jit(solution)/shard_map/ppermute | solution.py:46
  7.9 7.7 %collective-permute-done = f32[512,128]{1,0:T(8,128)S(1)} collective-permute-done((f32[512,128]{1,0:T(8,128)}, f32[512,128]{1,0:T(8,128)S(1)}, u32[]{:S(2)}, u32[]{:S(2)}) %collective-permute-start) | collective-permute-done | bytes 262176 | tf_op jit(solution)/shard_map/ppermute | solution.py:46
  19.5 5.7 %collective-permute-start.3 = (f32[512,512]{1,0:T(8,128)S(1)}, f32[512,512]{1,0:T(8,128)S(1)}, u32[]{:S(2)}, u32[]{:S(2)}) collective-permute-start(f32[512,512]{1,0:T(8,128)S(1)} %get-tuple-element.55.refs_6_.refs_8_), channel_id=1, source_target_pairs={{0,16},{8,60},{16,32},{24,8},{32,48},{40,24},{48,4},{56,40},{4,20}... | collective-permute-start | bytes 3145736 | tf_op jit(solution)/shard_map/ppermute | solution.py:32
  25.6 1.6 collective-permute-start.4
  27.2 12.7 %collective-permute-done.5 = f32[2,512,128]{2,1,0:T(8,128)S(1)} collective-permute-done((f32[2,512,128]{2,1,0:T(8,128)S(1)}, f32[2,512,128]{2,1,0:T(8,128)S(1)}, u32[]{:S(2)}, u32[]{:S(2)}) %collective-permute-start.5) | collective-permute-done | bytes 524320 | tf_op jit(solution)/shard_map/ppermute | solution.py:381
  41.3 2.2 collective-permute-start.7
  43.6 2.3 collective-permute-start.2
  45.9 11.8 %collective-permute-done.7 = f32[2,512,128]{2,1,0:T(8,128)S(1)} collective-permute-done((f32[2,512,128]{2,1,0:T(8,128)S(1)}, f32[2,512,128]{2,1,0:T(8,128)S(1)}, u32[]{:S(2)}, u32[]{:S(2)}) %collective-permute-start.7) | collective-permute-done | bytes 524320 | tf_op jit(solution)/shard_map/ppermute | solution.py:381
  59.2 9.1 %collective-permute-done.2.refs_1_ = f32[512,512]{1,0:T(8,128)S(1)} collective-permute-done((f32[512,512]{1,0:T(8,128)S(1)}, f32[512,512]{1,0:T(8,128)S(1)}, u32[]{:S(2)}, u32[]{:S(2)}) %collective-permute-start.2) | collective-permute-done | bytes 1048608 | tf_op jit(solution)/shard_map/ppermute | solution.py:37
  74.0 10.3 %collective-permute-done.10.refs_2_ = f32[512,512]{1,0:T(8,128)S(1)} collective-permute-done((f32[512,512]{1,0:T(8,128)S(1)}, f32[512,512]{1,0:T(8,128)S(1)}, u32[]{:S(2)}, u32[]{:S(2)}) %collective-permute-start.10) | collective-permute-done | bytes 1048608 | tf_op jit(solution)/shard_map/ppermute | solution.py:37
  84.5 11.2 %collective-permute-done.12.refs_3_ = f32[2,2,512,128]{3,2,1,0:T(8,128)S(1)} collective-permute-done((f32[2,2,512,128]{3,2,1,0:T(8,128)S(1)}, f32[2,2,512,128]{3,2,1,0:T(8,128)S(1)}, u32[]{:S(2)}, u32[]{:S(2)}) %collective-permute-start.12) | collective-permute-done | bytes 1048608 | tf_op jit(solution)/shard_map/ppermute | solution.py:42
  97.1 1.9 collective-permute-start.16
  99.0 2.6 %collective-permute-start.15 = (f32[512,512]{1,0:T(8,128)S(1)}, f32[512,512]{1,0:T(8,128)S(1)}, u32[]{:S(2)}, u32[]{:S(2)}) collective-permute-start(f32[512,512]{1,0:T(8,128)S(1)} %collective-permute-done.10.refs_2_), channel_id=1, source_target_pairs={{0,1},{8,11},{1,2},{9,8},{2,3},{10,9},{3,0},{11,10},{4,5},{12,15},... | collective-permute-start | bytes 3145736 | tf_op jit(solution)/shard_map/ppermute | solution.py:37
  101.6 1.5 collective-permute-start.17
  104.3 7.6 %collective-permute-done.13.refs_11_.refs_13_ = f32[512,512]{1,0:T(8,128)S(1)} collective-permute-done((f32[512,512]{1,0:T(8,128)S(1)}, f32[512,512]{1,0:T(8,128)S(1)}, u32[]{:S(2)}, u32[]{:S(2)}) %collective-permute-start.13) | collective-permute-done | bytes 1048608 | tf_op jit(solution)/shard_map/ppermute | solution.py:32
  112.0 11.2 %collective-permute-done.15.refs_3_ = f32[512,512]{1,0:T(8,128)S(1)} collective-permute-done((f32[512,512]{1,0:T(8,128)S(1)}, f32[512,512]{1,0:T(8,128)S(1)}, u32[]{:S(2)}, u32[]{:S(2)}) %collective-permute-start.15) | collective-permute-done | bytes 1048608 | tf_op jit(solution)/shard_map/ppermute | solution.py:37
  123.2 4.5 %collective-permute-done.18.refs_5_ = f32[2,2,512,128]{3,2,1,0:T(8,128)} collective-permute-done((f32[2,2,512,128]{3,2,1,0:T(8,128)S(1)}, f32[2,2,512,128]{3,2,1,0:T(8,128)}, u32[]{:S(2)}, u32[]{:S(2)}) %collective-permute-start.18) | collective-permute-done | bytes 1048608 | tf_op jit(solution)/shard_map/ppermute | solution.py:42
  128.1 2.1 collective-permute-start.19
  132.8 10.1 %collective-permute-done.19.refs_6_ = f32[512,512]{1,0:T(8,128)} collective-permute-done((f32[512,512]{1,0:T(8,128)S(1)}, f32[512,512]{1,0:T(8,128)}, u32[]{:S(2)}, u32[]{:S(2)}) %collective-permute-start.19) | collective-permute-done | bytes 1048608 | tf_op jit(solution)/shard_map/ppermute | solution.py:37
  143.0 2.1 collective-permute-start.21
  145.8 14.0 %shard_map.61 = (f32[2,512,512]{2,1,0:T(8,128)}, f32[2,512,512]{2,1,0:T(8,128)}) custom-call(s32[5]{0:T(128)} %stack.50.place, f32[2,2,512,128]{3,2,1,0:T(8,128)} %copy-done.9, f32[2,2,512,128]{3,2,1,0:T(8,128)} %copy-done.10, f32[2,2,512,128]{3,2,1,0:T(8,128)} %copy-done.20, f32[2,2,512,128]{3,2,1,0:T(8,128)} %copy-done.21, ...), custom_call_target="tpu_custom_call" | custom-call | flops 4831838208 | bytes 18874368 | tf_op jit(solution)/shard_map/pallas_call | solution.py:282
  159.9 13.5 %shard_map.62 = (f32[2,512,512]{2,1,0:T(8,128)}, f32[2,512,512]{2,1,0:T(8,128)}) custom-call(s32[5]{0:T(128)} %stack.50.place, f32[2,2,512,128]{3,2,1,0:T(8,128)} %copy-done.9, f32[2,2,512,128]{3,2,1,0:T(8,128)} %copy-done.10, f32[2,2,512,128]{3,2,1,0:T(8,128)} %copy-done.20, ...), custom_call_target="tpu_custom_call", output_to_operand_aliasing={{0}: (17, {}), {1}: (18, {})} | custom-call | flops 4831838208 | bytes 18874368 | tf_op jit(solution)/shard_map/pallas_call | solution.py:282
  173.4 4.4 %collective-permute-done.24.refs_9_ = f32[2,512,512]{2,1,0:T(8,128)S(1)} collective-permute-done((f32[2,512,512]{2,1,0:T(8,128)}, f32[2,512,512]{2,1,0:T(8,128)S(1)}, u32[]{:S(2)}, u32[]{:S(2)}) %collective-permute-start.24) | collective-permute-done | bytes 2097184 | tf_op jit(solution)/shard_map/ppermute | solution.py:46
  179.2 10.0 %shard_map.63 = (f32[2,512,512]{2,1,0:T(8,128)}, f32[256,512]{1,0:T(8,128)}, f32[256,512]{1,0:T(8,128)}, f32[256,512]{1,0:T(8,128)}, f32[256,512]{1,0:T(8,128)},...) custom-call(s32[5]{0:T(128)} %stack.50.place, f32[512,512]{1,0:T(8,128)} %copy-done.3, ...), custom_call_target="tpu_custom_call" | custom-call | flops 1610612736 | bytes 6291456 | tf_op jit(solution)/shard_map/pallas_call | solution.py:320
  193.8 2.4 %collective-permute-start.34 = (f32[256,512]{1,0:T(8,128)S(1)}, f32[256,512]{1,0:T(8,128)S(1)}, u32[]{:S(2)}, u32[]{:S(2)}) collective-permute-start(f32[256,512]{1,0:T(8,128)S(1)} %copy-done.31), channel_id=1, source_target_pairs={{0,8},{8,0},{1,9},{9,1},{2,10},{10,2},{3,11},{11,3},{4,12},{12,4},... | collective-permute-start | bytes 1572872 | tf_op jit(solution)/shard_map/ppermute | solution.py:46
  196.2 9.1 %shard_map.65 = (f32[256,512]{1,0:T(8,128)}, f32[256,512]{1,0:T(8,128)}, f32[256,512]{1,0:T(8,128)}, f32[256,512]{1,0:T(8,128)}, f32[256,512]{1,0:T(8,128)}, /*i...) custom-call(s32[5]{0:T(128)} %stack.50.place, f32[512,512]{1,0:T(8,128)} %copy-done.3, ...), custom_call_target="tpu_custom_call" | custom-call | tf_op jit(solution)/shard_map/pallas_call | solution.py:343
  207.6 2.2 collective-permute-done.33
  211.3 6.0 %collective-permute-done.29 = f32[256,512]{1,0:T(8,128)S(1)} collective-permute-done((f32[256,512]{1,0:T(8,128)S(1)}, f32[256,512]{1,0:T(8,128)S(1)}, u32[]{:S(2)}, u32[]{:S(2)}) %collective-permute-start.29) | collective-permute-done | bytes 524320 | tf_op jit(solution)/shard_map/ppermute | solution.py:32
  217.6 5.3 %collective-permute-done.35 = f32[256,512]{1,0:T(8,128)S(1)} collective-permute-done((f32[256,512]{1,0:T(8,128)S(1)}, f32[256,512]{1,0:T(8,128)S(1)}, u32[]{:S(2)}, u32[]{:S(2)}) %collective-permute-start.35) | collective-permute-done | bytes 524320 | tf_op jit(solution)/shard_map/ppermute | solution.py:32
  223.2 1.7 shard_map.64
  224.9 3.6 %collective-permute-done.31 = f32[256,512]{1,0:T(8,128)S(1)} collective-permute-done((f32[256,512]{1,0:T(8,128)S(1)}, f32[256,512]{1,0:T(8,128)S(1)}, u32[]{:S(2)}, u32[]{:S(2)}) %collective-permute-start.31) | collective-permute-done | bytes 524320 | tf_op jit(solution)/shard_map/ppermute | solution.py:32
  228.7 5.5 %collective-permute-done.37 = f32[256,512]{1,0:T(8,128)S(1)} collective-permute-done((f32[256,512]{1,0:T(8,128)S(1)}, f32[256,512]{1,0:T(8,128)S(1)}, u32[]{:S(2)}, u32[]{:S(2)}) %collective-permute-start.37) | collective-permute-done | bytes 524320 | tf_op jit(solution)/shard_map/ppermute | solution.py:32
  (131 shorter events, 31.4 us)
Async XLA Ops:
  0.6 14.9 %collective-permute-start = (f32[512,128]{1,0:T(8,128)}, f32[512,128]{1,0:T(8,128)S(1)}, u32[]{:S(2)}, u32[]{:S(2)}) collective-permute-start(f32[512,128]{1,0:T(8,128)} %param.4), channel_id=1, source_target_pairs={{0,4},{4,0},{1,5},{5,1},{2,6},{6,2},{3,7},{7,3},{8,12},{12,8},{9,1... | collective-permute-start | bytes 786440 | tf_op jit(solution)/shard_map/ppermute | solution.py:46
  19.5 21.8 %collective-permute-start.3 = (f32[512,512]{1,0:T(8,128)S(1)}, f32[512,512]{1,0:T(8,128)S(1)}, u32[]{:S(2)}, u32[]{:S(2)}) collective-permute-start(f32[512,512]{1,0:T(8,128)S(1)} %get-tuple-element.55.refs_6_.refs_8_), channel_id=1, source_target_pairs={{0,16},{8,60},{16,32},{24,8},{32,48},{40,24},{48,4},{56,40},{4,20}... | collective-permute-start | bytes 3145736 | tf_op jit(solution)/shard_map/ppermute | solution.py:32
  25.2 14.7 %collective-permute-start.5 = (f32[2,512,128]{2,1,0:T(8,128)S(1)}, f32[2,512,128]{2,1,0:T(8,128)S(1)}, u32[]{:S(2)}, u32[]{:S(2)}) collective-permute-start(f32[2,512,128]{2,1,0:T(8,128)S(1)} %pad_maximum_fusion.2), channel_id=1, source_target_pairs={{0,3},{1,0},{2,1},{3,2},{4,7},{5,4},{6,5},{7,6},{8,11},{9,8},{10,9... | collective-permute-start | bytes 1572872 | tf_op jit(solution)/shard_map/ppermute | solution.py:381
  25.6 15.7 %collective-permute-start.4 = (f32[2,512,128]{2,1,0:T(8,128)S(1)}, f32[2,512,128]{2,1,0:T(8,128)S(1)}, u32[]{:S(2)}, u32[]{:S(2)}) collective-permute-start(f32[2,512,128]{2,1,0:T(8,128)S(1)} %pad_maximum_fusion.2), channel_id=1, source_target_pairs={{0,1},{1,2},{2,3},{3,0},{4,5},{5,6},{6,7},{7,4},{8,9},{9,10},{10,1... | collective-permute-start | bytes 1572872 | tf_op jit(solution)/shard_map/ppermute | solution.py:381
  41.3 16.5 %collective-permute-start.6 = (f32[512,512]{1,0:T(8,128)S(1)}, f32[512,512]{1,0:T(8,128)S(1)}, u32[]{:S(2)}, u32[]{:S(2)}) collective-permute-start(f32[512,512]{1,0:T(8,128)S(1)} %collective-permute-done.3.refs_7_.refs_9_), channel_id=1, source_target_pairs={{0,16},{8,60},{16,32},{24,8},{32,48},{40,24},{48,4},{56,40},{4,20}... | collective-permute-start | bytes 3145736 | tf_op jit(solution)/shard_map/ppermute | solution.py:32
  41.3 16.3 %collective-permute-start.7 = (f32[2,512,128]{2,1,0:T(8,128)S(1)}, f32[2,512,128]{2,1,0:T(8,128)S(1)}, u32[]{:S(2)}, u32[]{:S(2)}) collective-permute-start(f32[2,512,128]{2,1,0:T(8,128)S(1)} %pad_maximum_fusion.2), channel_id=1, source_target_pairs={{0,2},{1,3},{2,0},{3,1},{4,6},{5,7},{6,4},{7,5},{8,10},{9,11},{10,... | collective-permute-start | bytes 1572872 | tf_op jit(solution)/shard_map/ppermute | solution.py:381
  43.6 24.7 %collective-permute-start.2 = (f32[512,512]{1,0:T(8,128)S(1)}, f32[512,512]{1,0:T(8,128)S(1)}, u32[]{:S(2)}, u32[]{:S(2)}) collective-permute-start(f32[512,512]{1,0:T(8,128)S(1)} %get-tuple-element.54.refs_0_), channel_id=1, source_target_pairs={{0,1},{8,11},{1,2},{9,8},{2,3},{10,9},{3,0},{11,10},{4,5},{12,15},... | collective-permute-start | bytes 3145736 | tf_op jit(solution)/shard_map/ppermute | solution.py:37
  57.8 16.1 %collective-permute-start.8 = (f32[512,512]{1,0:T(8,128)S(1)}, f32[512,512]{1,0:T(8,128)S(1)}, u32[]{:S(2)}, u32[]{:S(2)}) collective-permute-start(f32[512,512]{1,0:T(8,128)S(1)} %collective-permute-done.6.refs_8_.refs_10_), channel_id=1, source_target_pairs={{0,16},{8,60},{16,32},{24,8},{32,48},{40,24},{48,4},{56,40},{4,20}... | collective-permute-start | bytes 3145736 | tf_op jit(solution)/shard_map/ppermute | solution.py:32
  68.3 16.0 %collective-permute-start.10 = (f32[512,512]{1,0:T(8,128)S(1)}, f32[512,512]{1,0:T(8,128)S(1)}, u32[]{:S(2)}, u32[]{:S(2)}) collective-permute-start(f32[512,512]{1,0:T(8,128)S(1)} %collective-permute-done.2.refs_1_), channel_id=1, source_target_pairs={{0,1},{8,11},{1,2},{9,8},{2,3},{10,9},{3,0},{11,10},{4,5},{12,15},... | collective-permute-start | bytes 3145736 | tf_op jit(solution)/shard_map/ppermute | solution.py:37
  69.7 14.8 %collective-permute-start.11 = (f32[2,2,512,128]{3,2,1,0:T(8,128)S(1)}, f32[2,2,512,128]{3,2,1,0:T(8,128)S(1)}, u32[]{:S(2)}, u32[]{:S(2)}) collective-permute-start(f32[2,2,512,128]{3,2,1,0:T(8,128)S(1)} %pad_maximum_fusion.refs_0_), channel_id=1, source_target_pairs={{0,64},{8,200},{64,128},{72,8},{128,192},{136,72},{192,0},{200,136... | collective-permute-start | bytes 3145736 | tf_op jit(solution)/shard_map/ppermute | solution.py:42
  71.2 24.5 %collective-permute-start.12 = (f32[2,2,512,128]{3,2,1,0:T(8,128)S(1)}, f32[2,2,512,128]{3,2,1,0:T(8,128)S(1)}, u32[]{:S(2)}, u32[]{:S(2)}) collective-permute-start(f32[2,2,512,128]{3,2,1,0:T(8,128)S(1)} %pad_maximum_fusion.1.refs_1_), channel_id=1, source_target_pairs={{0,64},{8,200},{64,128},{72,8},{128,192},{136,72},{192,0},{200,136... | collective-permute-start | bytes 3145736 | tf_op jit(solution)/shard_map/ppermute | solution.py:42
  73.9 21.9 %collective-permute-start.9 = (f32[512,512]{1,0:T(8,128)S(1)}, f32[512,512]{1,0:T(8,128)S(1)}, u32[]{:S(2)}, u32[]{:S(2)}) collective-permute-start(f32[512,512]{1,0:T(8,128)S(1)} %collective-permute-done.8.refs_9_.refs_11_), channel_id=1, source_target_pairs={{0,16},{8,60},{16,32},{24,8},{32,48},{40,24},{48,4},{56,40},{4,20}... | collective-permute-start | bytes 3145736 | tf_op jit(solution)/shard_map/ppermute | solution.py:32
  95.8 16.1 %collective-permute-start.13 = (f32[512,512]{1,0:T(8,128)S(1)}, f32[512,512]{1,0:T(8,128)S(1)}, u32[]{:S(2)}, u32[]{:S(2)}) collective-permute-start(f32[512,512]{1,0:T(8,128)S(1)} %collective-permute-done.9.block.refs_10_.refs_12_), channel_id=1, source_target_pairs={{0,16},{8,60},{16,32},{24,8},{32,48},{40,24},{48,4},{56,40},{4,20}... | collective-permute-start | bytes 3145736 | tf_op jit(solution)/shard_map/ppermute | solution.py:32
  97.1 14.9 %collective-permute-start.16 = (f32[512,512]{1,0:T(8,128)S(1)}, f32[512,512]{1,0:T(8,128)S(1)}, u32[]{:S(2)}, u32[]{:S(2)}) collective-permute-start(f32[512,512]{1,0:T(8,128)S(1)} %shard_map.60.refs_4_), channel_id=1, source_target_pairs={{0,1},{8,11},{1,2},{9,8},{2,3},{10,9},{3,0},{11,10},{4,5},{12,15},... | collective-permute-start | bytes 3145736 | tf_op jit(solution)/shard_map/ppermute | solution.py:37
  99.0 24.2 %collective-permute-start.15 = (f32[512,512]{1,0:T(8,128)S(1)}, f32[512,512]{1,0:T(8,128)S(1)}, u32[]{:S(2)}, u32[]{:S(2)}) collective-permute-start(f32[512,512]{1,0:T(8,128)S(1)} %collective-permute-done.10.refs_2_), channel_id=1, source_target_pairs={{0,1},{8,11},{1,2},{9,8},{2,3},{10,9},{3,0},{11,10},{4,5},{12,15},... | collective-permute-start | bytes 3145736 | tf_op jit(solution)/shard_map/ppermute | solution.py:37
  101.6 21.6 %collective-permute-start.17 = (f32[2,2,512,128]{3,2,1,0:T(8,128)S(1)}, f32[2,2,512,128]{3,2,1,0:T(8,128)}, u32[]{:S(2)}, u32[]{:S(2)}) collective-permute-start(f32[2,2,512,128]{3,2,1,0:T(8,128)S(1)} %collective-permute-done.11.refs_2_), channel_id=1, source_target_pairs={{0,64},{8,200},{64,128},{72,8},{128,192},{136,72},{192,0},{200,136... | collective-permute-start | bytes 3145736 | tf_op jit(solution)/shard_map/ppermute | solution.py:42
  103.1 24.6 %collective-permute-start.18 = (f32[2,2,512,128]{3,2,1,0:T(8,128)S(1)}, f32[2,2,512,128]{3,2,1,0:T(8,128)}, u32[]{:S(2)}, u32[]{:S(2)}) collective-permute-start(f32[2,2,512,128]{3,2,1,0:T(8,128)S(1)} %collective-permute-done.12.refs_3_), channel_id=1, source_target_pairs={{0,64},{8,200},{64,128},{72,8},{128,192},{136,72},{192,0},{200,136... | collective-permute-start | bytes 3145736 | tf_op jit(solution)/shard_map/ppermute | solution.py:42
  111.9 16.1 %collective-permute-start.14 = (f32[512,512]{1,0:T(8,128)S(1)}, f32[512,512]{1,0:T(8,128)}, u32[]{:S(2)}, u32[]{:S(2)}) collective-permute-start(f32[512,512]{1,0:T(8,128)S(1)} %collective-permute-done.13.refs_11_.refs_13_), channel_id=1, source_target_pairs={{0,16},{8,60},{16,32},{24,8},{32,48},{40,24},{48,4},{56,40},{4,20}... | collective-permute-start | bytes 3145736 | tf_op jit(solution)/shard_map/ppermute | solution.py:32
  128.1 14.9 %collective-permute-start.19 = (f32[512,512]{1,0:T(8,128)S(1)}, f32[512,512]{1,0:T(8,128)}, u32[]{:S(2)}, u32[]{:S(2)}) collective-permute-start(f32[512,512]{1,0:T(8,128)S(1)} %collective-permute-done.16.refs_5_), channel_id=1, source_target_pairs={{0,1},{8,11},{1,2},{9,8},{2,3},{10,9},{3,0},{11,10},{4,5},{12,15},... | collective-permute-start | bytes 3145736 | tf_op jit(solution)/shard_map/ppermute | solution.py:37
  130.1 29.7 %collective-permute-start.22 = (f32[2,2,512,128]{3,2,1,0:T(8,128)}, f32[2,2,512,128]{3,2,1,0:T(8,128)}, u32[]{:S(2)}, u32[]{:S(2)}) collective-permute-start(f32[2,2,512,128]{3,2,1,0:T(8,128)} %collective-permute-done.17.refs_4_), channel_id=1, source_target_pairs={{0,64},{8,200},{64,128},{72,8},{128,192},{136,72},{192,0},{200,136... | collective-permute-start | bytes 3145736 | tf_op jit(solution)/shard_map/ppermute | solution.py:42
  131.6 28.2 %collective-permute-start.23 = (f32[2,2,512,128]{3,2,1,0:T(8,128)}, f32[2,2,512,128]{3,2,1,0:T(8,128)}, u32[]{:S(2)}, u32[]{:S(2)}) collective-permute-start(f32[2,2,512,128]{3,2,1,0:T(8,128)} %collective-permute-done.18.refs_5_), channel_id=1, source_target_pairs={{0,64},{8,200},{64,128},{72,8},{128,192},{136,72},{192,0},{200,136... | collective-permute-start | bytes 3145736 | tf_op jit(solution)/shard_map/ppermute | solution.py:42
  132.8 27.0 %collective-permute-start.20 = (f32[512,512]{1,0:T(8,128)}, f32[512,512]{1,0:T(8,128)}, u32[]{:S(2)}, u32[]{:S(2)}) collective-permute-start(f32[512,512]{1,0:T(8,128)} %collective-permute-done.14.refs_12_.refs_14_), channel_id=1, source_target_pairs={{0,16},{8,60},{16,32},{24,8},{32,48},{40,24},{48,4},{56,40},{4,20}... | collective-permute-start | bytes 3145736 | tf_op jit(solution)/shard_map/ppermute | solution.py:32
  143.0 16.9 %collective-permute-start.21 = (f32[512,512]{1,0:T(8,128)}, f32[512,512]{1,0:T(8,128)}, u32[]{:S(2)}, u32[]{:S(2)}) collective-permute-start(f32[512,512]{1,0:T(8,128)} %collective-permute-done.19.refs_6_), channel_id=1, source_target_pairs={{0,1},{8,11},{1,2},{9,8},{2,3},{10,9},{3,0},{11,10},{4,5},{12,15},... | collective-permute-start | bytes 3145736 | tf_op jit(solution)/shard_map/ppermute | solution.py:37
  189.8 16.8 %collective-permute-start.28 = (f32[256,512]{1,0:T(8,128)}, f32[256,512]{1,0:T(8,128)S(1)}, u32[]{:S(2)}, u32[]{:S(2)}) collective-permute-start(f32[256,512]{1,0:T(8,128)} %get-tuple-element.89), channel_id=1, source_target_pairs={{0,8},{8,0},{1,9},{9,1},{2,10},{10,2},{3,11},{11,3},{4,12},{12,4},... | collective-permute-start | bytes 1572872 | tf_op jit(solution)/shard_map/ppermute | solution.py:46
  193.7 13.0 %collective-permute-start.27 = (f32[256,512]{1,0:T(8,128)S(1)}, f32[256,512]{1,0:T(8,128)S(1)}, u32[]{:S(2)}, u32[]{:S(2)}) collective-permute-start(f32[256,512]{1,0:T(8,128)S(1)} %add.45), channel_id=1, source_target_pairs={{0,16},{8,60},{16,32},{24,8},{32,48},{40,24},{48,4},{56,40},{4,20}... | collective-permute-start | bytes 1572872 | tf_op jit(solution)/shard_map/ppermute | solution.py:32
  193.8 13.8 %collective-permute-start.34 = (f32[256,512]{1,0:T(8,128)S(1)}, f32[256,512]{1,0:T(8,128)S(1)}, u32[]{:S(2)}, u32[]{:S(2)}) collective-permute-start(f32[256,512]{1,0:T(8,128)S(1)} %copy-done.31), channel_id=1, source_target_pairs={{0,8},{8,0},{1,9},{9,1},{2,10},{10,2},{3,11},{11,3},{4,12},{12,4},... | collective-permute-start | bytes 1572872 | tf_op jit(solution)/shard_map/ppermute | solution.py:46
  196.1 13.6 %collective-permute-start.33 = (f32[256,512]{1,0:T(8,128)S(1)}, f32[256,512]{1,0:T(8,128)S(1)}, u32[]{:S(2)}, u32[]{:S(2)}) collective-permute-start(f32[256,512]{1,0:T(8,128)S(1)} %add.46), channel_id=1, source_target_pairs={{0,16},{8,60},{16,32},{24,8},{32,48},{40,24},{48,4},{56,40},{4,20}... | collective-permute-start | bytes 1572872 | tf_op jit(solution)/shard_map/ppermute | solution.py:32
  209.9 13.0 %collective-permute-start.35 = (f32[256,512]{1,0:T(8,128)S(1)}, f32[256,512]{1,0:T(8,128)S(1)}, u32[]{:S(2)}, u32[]{:S(2)}) collective-permute-start(f32[256,512]{1,0:T(8,128)S(1)} %add_add_fusion.2), channel_id=1, source_target_pairs={{0,16},{8,60},{16,32},{24,8},{32,48},{40,24},{48,4},{56,40},{4,20}... | collective-permute-start | bytes 1572872 | tf_op jit(solution)/shard_map/ppermute | solution.py:32
  210.0 14.9 %collective-permute-start.32 = (f32[256,512]{1,0:T(8,128)S(1)}, f32[256,512]{1,0:T(8,128)S(1)}, u32[]{:S(2)}, u32[]{:S(2)}) collective-permute-start(f32[256,512]{1,0:T(8,128)S(1)} %copy-done.30), channel_id=1, source_target_pairs={{0,8},{8,0},{1,9},{9,1},{2,10},{10,2},{3,11},{11,3},{4,12},{12,4},... | collective-permute-start | bytes 1572872 | tf_op jit(solution)/shard_map/ppermute | solution.py:46
  211.2 17.5 %collective-permute-start.38 = (f32[256,512]{1,0:T(8,128)S(1)}, f32[256,512]{1,0:T(8,128)S(1)}, u32[]{:S(2)}, u32[]{:S(2)}) collective-permute-start(f32[256,512]{1,0:T(8,128)S(1)} %copy-done.29), channel_id=1, source_target_pairs={{0,8},{8,0},{1,9},{9,1},{2,10},{10,2},{3,11},{11,3},{4,12},{12,4},... | collective-permute-start | bytes 1572872 | tf_op jit(solution)/shard_map/ppermute | solution.py:46
  217.5 11.1 %collective-permute-start.31 = (f32[256,512]{1,0:T(8,128)S(1)}, f32[256,512]{1,0:T(8,128)S(1)}, u32[]{:S(2)}, u32[]{:S(2)}) collective-permute-start(f32[256,512]{1,0:T(8,128)S(1)} %add_add_fusion.4), channel_id=1, source_target_pairs={{0,16},{8,60},{16,32},{24,8},{32,48},{40,24},{48,4},{56,40},{4,20}... | collective-permute-start | bytes 1572872 | tf_op jit(solution)/shard_map/ppermute | solution.py:32
  223.1 11.1 %collective-permute-start.37 = (f32[256,512]{1,0:T(8,128)S(1)}, f32[256,512]{1,0:T(8,128)S(1)}, u32[]{:S(2)}, u32[]{:S(2)}) collective-permute-start(f32[256,512]{1,0:T(8,128)S(1)} %add_add_fusion.1), channel_id=1, source_target_pairs={{0,16},{8,60},{16,32},{24,8},{32,48},{40,24},{48,4},{56,40},{4,20}... | collective-permute-start | bytes 1572872 | tf_op jit(solution)/shard_map/ppermute | solution.py:32
  (39 other events, 860.4 us)
where the time goes:
time: 239 us; the launch traced here: 236 us
  waiting for transfers between devices  128 us (54%)
  Pallas kernels  49.5 us (21%)
  starting transfers between devices  47.2 us (20%)
  other arithmetic  5.46 us (2%)
  local copies, waits for them, and re-layouts  4.05 us (2%)
    ppermute x6, waiting for transfers between devices, y_step(): return lax.ppermute(block, ('core', 'y'), pairs)  40.8 us
    ppermute x13, waiting for transfers between devices, z_step(): return lax.ppermute(block, ('z_lo', 'core', 'z_hi'), pairs)  32 us
    pallas_call x2, Pallas kernels, accumulate(): pl.pallas_call(functools.partial(gather_kernel, have, had), out_shape=(sh...  27.4 us
    ppermute x3, waiting for transfers between devices, from_all_y(): lax.ppermute(part, 'y', [(y, (y + k) % NY) for y in range(NY)])  25.9 us
    ppermute x6, waiting for transfers between devices, x_step(): return lax.ppermute(block, ('leaf', 'core'), pairs)  16 us
    ppermute x11, waiting for transfers between devices, swap(): return lax.ppermute(block, axis, [(0, 1), (1, 0)])  13.5 us
    ppermute x11, starting transfers between devices, swap(): return lax.ppermute(block, axis, [(0, 1), (1, 0)])  13.3 us
    ppermute x6, starting transfers between devices, y_step(): return lax.ppermute(block, ('core', 'y'), pairs)  12.4 us
  transfers between devices with their start and end apart: 39, of which 22 were waited for; matrix products, arithmetic and copies ran while one was open for 2% of the time, Pallas kernels for 11%

commit v1 on v0

--- a/solution.py
+++ b/solution.py
@@ -389,9 +389,10 @@
 
     good = core == zh
     kept, sent = jnp.where(good, root_inverse, away), jnp.where(good, away, root_inverse)
-    piece, mine, turned = lax.optimization_barrier((jnp.stack([kept, swap(sent, "core")]), mine, turned))
-
-    ring, rows_near, rows_far = [mine], [turned], []
+    piece = jnp.stack([kept, swap(sent, "core")])
+    piece, mine, moved = lax.optimization_barrier((piece, mine, y_step(turned)))
+
+    ring, rows_near, rows_far = [mine], [turned, moved], []
     had, totals = (0, 0), ()
     for r in range(NX):
         ends = [ring]
@@ -406,11 +407,11 @@
         else:
             for group in groups_of:
                 group.append(x_step(group[-1]))
-            for _ in range(2):
-                rows = rows_near if len(rows_near) < NY else rows_far
+            rows = rows_near if r == 1 else rows_far
+            for _ in range(min(2, NY - len(rows))):
                 rows.append(y_step(rows[-1]))
-            ends += [rows_near] if r == 1 else [rows_near, rows_far] if r == 2 else [rows_far]
-        ends += groups_of
+            ends.append(rows)
+        ends += groups_of + ([rows_near] if r == 0 else [])
         values = [into[-1] for into in ends]
         if r == NX - 1:
             had = (NX - 1, NZ - 1)

time: 239 us -> 232 us (0.971); the launches traced: 236 us -> 232 us
  starting transfers between devices: 47.2 us -> 38.6 us
  waiting for transfers between devices: 128 us -> 132 us
    ppermute x6, waiting for transfers between devices: 16 us -> 29.9 us  [x_step(): return lax.ppermute(block, ('leaf', 'core'), pairs)]
    ppermute x6, waiting for transfers between devices: 40.8 us -> 30.8 us  [y_step(): return lax.ppermute(block, ('core', 'y'), pairs)]
    ppermute x6, starting transfers between devices: 12.4 us -> 7.5 us  [y_step(): return lax.ppermute(block, ('core', 'y'), pairs)]
    ppermute x13, waiting for transfers between devices: 32 us -> 27.9 us  [z_step(): return lax.ppermute(block, ('z_lo', 'core', 'z_hi'), pairs)]
    ppermute x3, waiting for transfers between devices: 25.9 us -> 29.6 us  [from_all_y(): lax.ppermute(part, 'y', [(y, (y + k) % NY) for y in range(NY)])]
    ppermute x11, starting transfers between devices: 13.3 us -> 10.7 us  [swap(): return lax.ppermute(block, axis, [(0, 1), (1, 0)])]
  transfers between devices with their start and end apart: 39 -> 39, of which waited for: 22 -> 23; matrix products, arithmetic and copies ran while one was open for 2% -> 2% of each run, Pallas kernels for 11% -> 11%
where the time goes in v1:
time: 232 us
  waiting for transfers between devices  132 us (57%)
  Pallas kernels  49.5 us (21%)
  starting transfers between devices  38.6 us (17%)
  other arithmetic  5.46 us (2%)
  local copies, waits for them, and re-layouts  5.1 us (2%)
    ppermute x6, waiting for transfers between devices, y_step(): return lax.ppermute(block, ('core', 'y'), pairs)  30.8 us
    ppermute x6, waiting for transfers between devices, x_step(): return lax.ppermute(block, ('leaf', 'core'), pairs)  29.9 us
    ppermute x3, waiting for transfers between devices, from_all_y(): lax.ppermute(part, 'y', [(y, (y + k) % NY) for y in range(NY)])  29.6 us
    ppermute x13, waiting for transfers between devices, z_step(): return lax.ppermute(block, ('z_lo', 'core', 'z_hi'), pairs)  27.9 us
    pallas_call x2, Pallas kernels, accumulate(): pl.pallas_call(functools.partial(gather_kernel, have, had), out_shape=(sh...  27.4 us
    ppermute x11, waiting for transfers between devices, swap(): return lax.ppermute(block, axis, [(0, 1), (1, 0)])  13.6 us
    ppermute x11, starting transfers between devices, swap(): return lax.ppermute(block, axis, [(0, 1), (1, 0)])  10.7 us
    pallas_call x1, Pallas kernels, first_pairs(): pl.pallas_call(body, out_shape=(shaped(2, n, n),) + (shaped(n // 2, n),)...  10 us
  transfers between devices with their start and end apart: 39, of which 23 were waited for; matrix products, arithmetic and copies ran while one was open for 2% of the time, Pallas kernels for 11%

profile of v1, /device:TPU:10, one launch (start us, length us, event | category | flops | bytes accessed | tf_op | source)
XLA Modules:
  0.0 231.6 jit_solution(18408546144081664592)
XLA Ops:
  3.4 1.7 collective-permute-start.2
  5.1 7.2 %collective-permute-start = (f32[512,128]{1,0:T(8,128)}, f32[512,128]{1,0:T(8,128)S(1)}, u32[]{:S(2)}, u32[]{:S(2)}) collective-permute-start(f32[512,128]{1,0:T(8,128)} %param.4), channel_id=1, source_target_pairs={{0,4},{4,0},{1,5},{5,1},{2,6},{6,2},{3,7},{7,3},{8,12},{12,8},{9,1... | collective-permute-start | bytes 786440 | tf_op jit(solution)/shard_map/ppermute | solution.py:46
  12.3 6.2 %collective-permute-done = f32[512,128]{1,0:T(8,128)S(1)} collective-permute-done((f32[512,128]{1,0:T(8,128)}, f32[512,128]{1,0:T(8,128)S(1)}, u32[]{:S(2)}, u32[]{:S(2)}) %collective-permute-start) | collective-permute-done | bytes 262176 | tf_op jit(solution)/shard_map/ppermute | solution.py:46
  19.6 1.5 collective-permute-done.1
  21.2 5.7 %collective-permute-start.3 = (f32[512,512]{1,0:T(8,128)S(1)}, f32[512,512]{1,0:T(8,128)S(1)}, u32[]{:S(2)}, u32[]{:S(2)}) collective-permute-start(f32[512,512]{1,0:T(8,128)S(1)} %get-tuple-element.54.refs_6_.refs_8_), channel_id=1, source_target_pairs={{0,16},{8,60},{16,32},{24,8},{32,48},{40,24},{48,4},{56,40},{4,20}... | collective-permute-start | bytes 3145736 | tf_op jit(solution)/shard_map/ppermute | solution.py:32
  26.9 2.4 %collective-permute-start.5 = (f32[2,512,128]{2,1,0:T(8,128)S(1)}, f32[2,512,128]{2,1,0:T(8,128)S(1)}, u32[]{:S(2)}, u32[]{:S(2)}) collective-permute-start(f32[2,512,128]{2,1,0:T(8,128)S(1)} %pad_maximum_fusion.2), channel_id=1, source_target_pairs={{0,3},{1,0},{2,1},{3,2},{4,7},{5,4},{6,5},{7,6},{8,11},{9,8},{10,9... | collective-permute-start | bytes 1572872 | tf_op jit(solution)/shard_map/ppermute | solution.py:381
  29.3 12.2 %collective-permute-done.5 = f32[2,512,128]{2,1,0:T(8,128)S(1)} collective-permute-done((f32[2,512,128]{2,1,0:T(8,128)S(1)}, f32[2,512,128]{2,1,0:T(8,128)S(1)}, u32[]{:S(2)}, u32[]{:S(2)}) %collective-permute-start.5) | collective-permute-done | bytes 524320 | tf_op jit(solution)/shard_map/ppermute | solution.py:381
  41.5 2.4 %collective-permute-done.4 = f32[2,512,128]{2,1,0:T(8,128)S(1)} collective-permute-done((f32[2,512,128]{2,1,0:T(8,128)S(1)}, f32[2,512,128]{2,1,0:T(8,128)S(1)}, u32[]{:S(2)}, u32[]{:S(2)}) %collective-permute-start.4) | collective-permute-done | bytes 524320 | tf_op jit(solution)/shard_map/ppermute | solution.py:381
  45.3 14.9 %collective-permute-done.7 = f32[2,512,128]{2,1,0:T(8,128)S(1)} collective-permute-done((f32[2,512,128]{2,1,0:T(8,128)S(1)}, f32[2,512,128]{2,1,0:T(8,128)S(1)}, u32[]{:S(2)}, u32[]{:S(2)}) %collective-permute-start.7) | collective-permute-done | bytes 524320 | tf_op jit(solution)/shard_map/ppermute | solution.py:381
  64.1 11.2 %collective-permute-done.8.refs_2_ = f32[512,512]{1,0:T(8,128)S(1)} collective-permute-done((f32[512,512]{1,0:T(8,128)S(1)}, f32[512,512]{1,0:T(8,128)S(1)}, u32[]{:S(2)}, u32[]{:S(2)}) %collective-permute-start.8) | collective-permute-done | bytes 1048608 | tf_op jit(solution)/shard_map/ppermute | solution.py:37
  76.5 10.9 %collective-permute-done.13.refs_3_ = f32[2,2,512,128]{3,2,1,0:T(8,128)S(1)} collective-permute-done((f32[2,2,512,128]{3,2,1,0:T(8,128)S(1)}, f32[2,2,512,128]{3,2,1,0:T(8,128)S(1)}, u32[]{:S(2)}, u32[]{:S(2)}) %collective-permute-start.13) | collective-permute-done | bytes 1048608 | tf_op jit(solution)/shard_map/ppermute | solution.py:42
  87.4 3.8 %collective-permute-done.11.refs_3_ = f32[512,512]{1,0:T(8,128)S(1)} collective-permute-done((f32[512,512]{1,0:T(8,128)S(1)}, f32[512,512]{1,0:T(8,128)S(1)}, u32[]{:S(2)}, u32[]{:S(2)}) %collective-permute-start.11) | collective-permute-done | bytes 1048608 | tf_op jit(solution)/shard_map/ppermute | solution.py:37
  92.9 1.6 collective-permute-start.14
  97.2 11.5 %collective-permute-done.14.refs_5_ = f32[512,512]{1,0:T(8,128)S(1)} collective-permute-done((f32[512,512]{1,0:T(8,128)S(1)}, f32[512,512]{1,0:T(8,128)S(1)}, u32[]{:S(2)}, u32[]{:S(2)}) %collective-permute-start.14) | collective-permute-done | bytes 1048608 | tf_op jit(solution)/shard_map/ppermute | solution.py:37
  110.5 10.1 %collective-permute-done.19.refs_5_ = f32[2,2,512,128]{3,2,1,0:T(8,128)} collective-permute-done((f32[2,2,512,128]{3,2,1,0:T(8,128)S(1)}, f32[2,2,512,128]{3,2,1,0:T(8,128)}, u32[]{:S(2)}, u32[]{:S(2)}) %collective-permute-start.19) | collective-permute-done | bytes 1048608 | tf_op jit(solution)/shard_map/ppermute | solution.py:42
  120.7 4.2 %collective-permute-done.17.refs_6_ = f32[512,512]{1,0:T(8,128)} collective-permute-done((f32[512,512]{1,0:T(8,128)S(1)}, f32[512,512]{1,0:T(8,128)}, u32[]{:S(2)}, u32[]{:S(2)}) %collective-permute-start.17) | collective-permute-done | bytes 1048608 | tf_op jit(solution)/shard_map/ppermute | solution.py:37
  124.9 1.8 collective-permute-done.16.refs_12_.refs_14_
  126.6 3.0 %collective-permute-start.21 = (f32[512,512]{1,0:T(8,128)}, f32[512,512]{1,0:T(8,128)}, u32[]{:S(2)}, u32[]{:S(2)}) collective-permute-start(f32[512,512]{1,0:T(8,128)} %collective-permute-done.17.refs_6_), channel_id=1, source_target_pairs={{0,1},{8,11},{1,2},{9,8},{2,3},{10,9},{3,0},{11,10},{4,5},{12,15},... | collective-permute-start | bytes 3145736 | tf_op jit(solution)/shard_map/ppermute | solution.py:37
  133.1 14.0 %shard_map.61 = (f32[2,512,512]{2,1,0:T(8,128)}, f32[2,512,512]{2,1,0:T(8,128)}) custom-call(s32[5]{0:T(128)} %stack.50.place, f32[2,2,512,128]{3,2,1,0:T(8,128)} %copy-done.9, f32[2,2,512,128]{3,2,1,0:T(8,128)} %copy-done.10, f32[2,2,512,128]{3,2,1,0:T(8,128)} %copy-done.20, f32[2,2,512,128]{3,2,1,0:T(8,128)} %copy-done.21, ...), custom_call_target="tpu_custom_call" | custom-call | flops 4831838208 | bytes 18874368 | tf_op jit(solution)/shard_map/pallas_call | solution.py:282
  147.1 8.9 %collective-permute-done.23.refs_7_ = f32[2,2,512,128]{3,2,1,0:T(8,128)} collective-permute-done((f32[2,2,512,128]{3,2,1,0:T(8,128)}, f32[2,2,512,128]{3,2,1,0:T(8,128)}, u32[]{:S(2)}, u32[]{:S(2)}) %collective-permute-start.23) | collective-permute-done | bytes 1048608 | tf_op jit(solution)/shard_map/ppermute | solution.py:42
  156.0 13.5 %shard_map.62 = (f32[2,512,512]{2,1,0:T(8,128)}, f32[2,512,512]{2,1,0:T(8,128)}) custom-call(s32[5]{0:T(128)} %stack.50.place, f32[2,2,512,128]{3,2,1,0:T(8,128)} %copy-done.9, f32[2,2,512,128]{3,2,1,0:T(8,128)} %copy-done.10, f32[2,2,512,128]{3,2,1,0:T(8,128)} %copy-done.20, ...), custom_call_target="tpu_custom_call", output_to_operand_aliasing={{0}: (17, {}), {1}: (18, {})} | custom-call | flops 4831838208 | bytes 18874368 | tf_op jit(solution)/shard_map/pallas_call | solution.py:282
  169.6 4.4 %collective-permute-done.24.refs_9_ = f32[2,512,512]{2,1,0:T(8,128)S(1)} collective-permute-done((f32[2,512,512]{2,1,0:T(8,128)}, f32[2,512,512]{2,1,0:T(8,128)S(1)}, u32[]{:S(2)}, u32[]{:S(2)}) %collective-permute-start.24) | collective-permute-done | bytes 2097184 | tf_op jit(solution)/shard_map/ppermute | solution.py:46
  175.3 10.0 %shard_map.63 = (f32[2,512,512]{2,1,0:T(8,128)}, f32[256,512]{1,0:T(8,128)}, f32[256,512]{1,0:T(8,128)}, f32[256,512]{1,0:T(8,128)}, f32[256,512]{1,0:T(8,128)},...) custom-call(s32[5]{0:T(128)} %stack.50.place, f32[512,512]{1,0:T(8,128)} %copy-done.3, ...), custom_call_target="tpu_custom_call" | custom-call | flops 1610612736 | bytes 6291456 | tf_op jit(solution)/shard_map/pallas_call | solution.py:320
  190.2 1.6 collective-permute-start.33
  191.8 9.1 %shard_map.65 = (f32[256,512]{1,0:T(8,128)}, f32[256,512]{1,0:T(8,128)}, f32[256,512]{1,0:T(8,128)}, f32[256,512]{1,0:T(8,128)}, f32[256,512]{1,0:T(8,128)}, /*i...) custom-call(s32[5]{0:T(128)} %stack.50.place, f32[512,512]{1,0:T(8,128)} %copy-done.3, ...), custom_call_target="tpu_custom_call" | custom-call | tf_op jit(solution)/shard_map/pallas_call | solution.py:343
  200.9 1.7 collective-permute-start.30
  203.0 2.9 %collective-permute-done.33 = f32[256,512]{1,0:T(8,128)S(1)} collective-permute-done((f32[256,512]{1,0:T(8,128)S(1)}, f32[256,512]{1,0:T(8,128)S(1)}, u32[]{:S(2)}, u32[]{:S(2)}) %collective-permute-start.33) | collective-permute-done | bytes 524320 | tf_op jit(solution)/shard_map/ppermute | solution.py:32
  206.8 6.6 %collective-permute-done.29 = f32[256,512]{1,0:T(8,128)S(1)} collective-permute-done((f32[256,512]{1,0:T(8,128)S(1)}, f32[256,512]{1,0:T(8,128)S(1)}, u32[]{:S(2)}, u32[]{:S(2)}) %collective-permute-start.29) | collective-permute-done | bytes 524320 | tf_op jit(solution)/shard_map/ppermute | solution.py:32
  213.6 5.3 %collective-permute-done.35 = f32[256,512]{1,0:T(8,128)S(1)} collective-permute-done((f32[256,512]{1,0:T(8,128)S(1)}, f32[256,512]{1,0:T(8,128)S(1)}, u32[]{:S(2)}, u32[]{:S(2)}) %collective-permute-start.35) | collective-permute-done | bytes 524320 | tf_op jit(solution)/shard_map/ppermute | solution.py:32
  219.3 1.7 shard_map.64
  221.0 3.6 %collective-permute-done.31 = f32[256,512]{1,0:T(8,128)S(1)} collective-permute-done((f32[256,512]{1,0:T(8,128)S(1)}, f32[256,512]{1,0:T(8,128)S(1)}, u32[]{:S(2)}, u32[]{:S(2)}) %collective-permute-start.31) | collective-permute-done | bytes 524320 | tf_op jit(solution)/shard_map/ppermute | solution.py:32
  224.8 5.5 %collective-permute-done.37 = f32[256,512]{1,0:T(8,128)S(1)} collective-permute-done((f32[256,512]{1,0:T(8,128)S(1)}, f32[256,512]{1,0:T(8,128)S(1)}, u32[]{:S(2)}, u32[]{:S(2)}) %collective-permute-start.37) | collective-permute-done | bytes 524320 | tf_op jit(solution)/shard_map/ppermute | solution.py:32
  (131 shorter events, 29.2 us)
Async XLA Ops:
  3.4 17.7 %collective-permute-start.2 = (f32[512,512]{1,0:T(8,128)S(1)}, f32[512,512]{1,0:T(8,128)S(1)}, u32[]{:S(2)}, u32[]{:S(2)}) collective-permute-start(f32[512,512]{1,0:T(8,128)S(1)} %get-tuple-element.52.refs_0_), channel_id=1, source_target_pairs={{0,1},{8,11},{1,2},{9,8},{2,3},{10,9},{3,0},{11,10},{4,5},{12,15},... | collective-permute-start | bytes 3145736 | tf_op jit(solution)/shard_map/ppermute | solution.py:37
  5.1 13.4 %collective-permute-start = (f32[512,128]{1,0:T(8,128)}, f32[512,128]{1,0:T(8,128)S(1)}, u32[]{:S(2)}, u32[]{:S(2)}) collective-permute-start(f32[512,128]{1,0:T(8,128)} %param.4), channel_id=1, source_target_pairs={{0,4},{4,0},{1,5},{5,1},{2,6},{6,2},{3,7},{7,3},{8,12},{12,8},{9,1... | collective-permute-start | bytes 786440 | tf_op jit(solution)/shard_map/ppermute | solution.py:46
  21.2 22.7 %collective-permute-start.3 = (f32[512,512]{1,0:T(8,128)S(1)}, f32[512,512]{1,0:T(8,128)S(1)}, u32[]{:S(2)}, u32[]{:S(2)}) collective-permute-start(f32[512,512]{1,0:T(8,128)S(1)} %get-tuple-element.54.refs_6_.refs_8_), channel_id=1, source_target_pairs={{0,16},{8,60},{16,32},{24,8},{32,48},{40,24},{48,4},{56,40},{4,20}... | collective-permute-start | bytes 3145736 | tf_op jit(solution)/shard_map/ppermute | solution.py:32
  26.9 14.6 %collective-permute-start.5 = (f32[2,512,128]{2,1,0:T(8,128)S(1)}, f32[2,512,128]{2,1,0:T(8,128)S(1)}, u32[]{:S(2)}, u32[]{:S(2)}) collective-permute-start(f32[2,512,128]{2,1,0:T(8,128)S(1)} %pad_maximum_fusion.2), channel_id=1, source_target_pairs={{0,3},{1,0},{2,1},{3,2},{4,7},{5,4},{6,5},{7,6},{8,11},{9,8},{10,9... | collective-permute-start | bytes 1572872 | tf_op jit(solution)/shard_map/ppermute | solution.py:381
  29.3 14.6 %collective-permute-start.4 = (f32[2,512,128]{2,1,0:T(8,128)S(1)}, f32[2,512,128]{2,1,0:T(8,128)S(1)}, u32[]{:S(2)}, u32[]{:S(2)}) collective-permute-start(f32[2,512,128]{2,1,0:T(8,128)S(1)} %pad_maximum_fusion.2), channel_id=1, source_target_pairs={{0,1},{1,2},{2,3},{3,0},{4,5},{5,6},{6,7},{7,4},{8,9},{9,10},{10,1... | collective-permute-start | bytes 1572872 | tf_op jit(solution)/shard_map/ppermute | solution.py:381
  43.9 16.4 %collective-permute-start.6 = (f32[512,512]{1,0:T(8,128)S(1)}, f32[512,512]{1,0:T(8,128)S(1)}, u32[]{:S(2)}, u32[]{:S(2)}) collective-permute-start(f32[512,512]{1,0:T(8,128)S(1)} %collective-permute-done.3.refs_7_.refs_9_), channel_id=1, source_target_pairs={{0,16},{8,60},{16,32},{24,8},{32,48},{40,24},{48,4},{56,40},{4,20}... | collective-permute-start | bytes 3145736 | tf_op jit(solution)/shard_map/ppermute | solution.py:32
  43.9 16.3 %collective-permute-start.7 = (f32[2,512,128]{2,1,0:T(8,128)S(1)}, f32[2,512,128]{2,1,0:T(8,128)S(1)}, u32[]{:S(2)}, u32[]{:S(2)}) collective-permute-start(f32[2,512,128]{2,1,0:T(8,128)S(1)} %pad_maximum_fusion.2), channel_id=1, source_target_pairs={{0,2},{1,3},{2,0},{3,1},{4,6},{5,7},{6,4},{7,5},{8,10},{9,11},{10,... | collective-permute-start | bytes 1572872 | tf_op jit(solution)/shard_map/ppermute | solution.py:381
  60.3 14.9 %collective-permute-start.8 = (f32[512,512]{1,0:T(8,128)S(1)}, f32[512,512]{1,0:T(8,128)S(1)}, u32[]{:S(2)}, u32[]{:S(2)}) collective-permute-start(f32[512,512]{1,0:T(8,128)S(1)} %collective-permute-done.2.refs_1_), channel_id=1, source_target_pairs={{0,1},{8,11},{1,2},{9,8},{2,3},{10,9},{3,0},{11,10},{4,5},{12,15},... | collective-permute-start | bytes 3145736 | tf_op jit(solution)/shard_map/ppermute | solution.py:37
  60.4 16.1 %collective-permute-start.9 = (f32[512,512]{1,0:T(8,128)S(1)}, f32[512,512]{1,0:T(8,128)S(1)}, u32[]{:S(2)}, u32[]{:S(2)}) collective-permute-start(f32[512,512]{1,0:T(8,128)S(1)} %collective-permute-done.6.refs_8_.refs_10_), channel_id=1, source_target_pairs={{0,16},{8,60},{16,32},{24,8},{32,48},{40,24},{48,4},{56,40},{4,20}... | collective-permute-start | bytes 3145736 | tf_op jit(solution)/shard_map/ppermute | solution.py:32
  61.4 15.2 %collective-permute-start.12 = (f32[2,2,512,128]{3,2,1,0:T(8,128)S(1)}, f32[2,2,512,128]{3,2,1,0:T(8,128)S(1)}, u32[]{:S(2)}, u32[]{:S(2)}) collective-permute-start(f32[2,2,512,128]{3,2,1,0:T(8,128)S(1)} %pad_maximum_fusion.refs_0_), channel_id=1, source_target_pairs={{0,64},{8,200},{64,128},{72,8},{128,192},{136,72},{192,0},{200,136... | collective-permute-start | bytes 3145736 | tf_op jit(solution)/shard_map/ppermute | solution.py:42
  62.9 24.5 %collective-permute-start.13 = (f32[2,2,512,128]{3,2,1,0:T(8,128)S(1)}, f32[2,2,512,128]{3,2,1,0:T(8,128)S(1)}, u32[]{:S(2)}, u32[]{:S(2)}) collective-permute-start(f32[2,2,512,128]{3,2,1,0:T(8,128)S(1)} %pad_maximum_fusion.1.refs_1_), channel_id=1, source_target_pairs={{0,64},{8,200},{64,128},{72,8},{128,192},{136,72},{192,0},{200,136... | collective-permute-start | bytes 3145736 | tf_op jit(solution)/shard_map/ppermute | solution.py:42
  75.2 16.0 %collective-permute-start.11 = (f32[512,512]{1,0:T(8,128)S(1)}, f32[512,512]{1,0:T(8,128)S(1)}, u32[]{:S(2)}, u32[]{:S(2)}) collective-permute-start(f32[512,512]{1,0:T(8,128)S(1)} %collective-permute-done.8.refs_2_), channel_id=1, source_target_pairs={{0,1},{8,11},{1,2},{9,8},{2,3},{10,9},{3,0},{11,10},{4,5},{12,15},... | collective-permute-start | bytes 3145736 | tf_op jit(solution)/shard_map/ppermute | solution.py:37
  76.5 16.0 %collective-permute-start.10 = (f32[512,512]{1,0:T(8,128)S(1)}, f32[512,512]{1,0:T(8,128)S(1)}, u32[]{:S(2)}, u32[]{:S(2)}) collective-permute-start(f32[512,512]{1,0:T(8,128)S(1)} %collective-permute-done.9.refs_9_.refs_11_), channel_id=1, source_target_pairs={{0,16},{8,60},{16,32},{24,8},{32,48},{40,24},{48,4},{56,40},{4,20}... | collective-permute-start | bytes 3145736 | tf_op jit(solution)/shard_map/ppermute | solution.py:32
  92.9 15.9 %collective-permute-start.14 = (f32[512,512]{1,0:T(8,128)S(1)}, f32[512,512]{1,0:T(8,128)S(1)}, u32[]{:S(2)}, u32[]{:S(2)}) collective-permute-start(f32[512,512]{1,0:T(8,128)S(1)} %shard_map.60.refs_4_), channel_id=1, source_target_pairs={{0,1},{8,11},{1,2},{9,8},{2,3},{10,9},{3,0},{11,10},{4,5},{12,15},... | collective-permute-start | bytes 3145736 | tf_op jit(solution)/shard_map/ppermute | solution.py:37
  94.5 16.0 %collective-permute-start.15 = (f32[512,512]{1,0:T(8,128)S(1)}, f32[512,512]{1,0:T(8,128)S(1)}, u32[]{:S(2)}, u32[]{:S(2)}) collective-permute-start(f32[512,512]{1,0:T(8,128)S(1)} %collective-permute-done.10.block.refs_10_.refs_12_), channel_id=1, source_target_pairs={{0,16},{8,60},{16,32},{24,8},{32,48},{40,24},{48,4},{56,40},{4,20}... | collective-permute-start | bytes 3145736 | tf_op jit(solution)/shard_map/ppermute | solution.py:32
  94.5 16.0 %collective-permute-start.18 = (f32[2,2,512,128]{3,2,1,0:T(8,128)S(1)}, f32[2,2,512,128]{3,2,1,0:T(8,128)}, u32[]{:S(2)}, u32[]{:S(2)}) collective-permute-start(f32[2,2,512,128]{3,2,1,0:T(8,128)S(1)} %collective-permute-done.12.refs_2_), channel_id=1, source_target_pairs={{0,64},{8,200},{64,128},{72,8},{128,192},{136,72},{192,0},{200,136... | collective-permute-start | bytes 3145736 | tf_op jit(solution)/shard_map/ppermute | solution.py:42
  96.0 24.6 %collective-permute-start.19 = (f32[2,2,512,128]{3,2,1,0:T(8,128)S(1)}, f32[2,2,512,128]{3,2,1,0:T(8,128)}, u32[]{:S(2)}, u32[]{:S(2)}) collective-permute-start(f32[2,2,512,128]{3,2,1,0:T(8,128)S(1)} %collective-permute-done.13.refs_3_), channel_id=1, source_target_pairs={{0,64},{8,200},{64,128},{72,8},{128,192},{136,72},{192,0},{200,136... | collective-permute-start | bytes 3145736 | tf_op jit(solution)/shard_map/ppermute | solution.py:42
  108.8 16.1 %collective-permute-start.17 = (f32[512,512]{1,0:T(8,128)S(1)}, f32[512,512]{1,0:T(8,128)}, u32[]{:S(2)}, u32[]{:S(2)}) collective-permute-start(f32[512,512]{1,0:T(8,128)S(1)} %collective-permute-done.14.refs_5_), channel_id=1, source_target_pairs={{0,1},{8,11},{1,2},{9,8},{2,3},{10,9},{3,0},{11,10},{4,5},{12,15},... | collective-permute-start | bytes 3145736 | tf_op jit(solution)/shard_map/ppermute | solution.py:37
  110.5 16.1 %collective-permute-start.16 = (f32[512,512]{1,0:T(8,128)S(1)}, f32[512,512]{1,0:T(8,128)}, u32[]{:S(2)}, u32[]{:S(2)}) collective-permute-start(f32[512,512]{1,0:T(8,128)S(1)} %collective-permute-done.15.refs_11_.refs_13_), channel_id=1, source_target_pairs={{0,16},{8,60},{16,32},{24,8},{32,48},{40,24},{48,4},{56,40},{4,20}... | collective-permute-start | bytes 3145736 | tf_op jit(solution)/shard_map/ppermute | solution.py:32
  126.6 20.4 %collective-permute-start.21 = (f32[512,512]{1,0:T(8,128)}, f32[512,512]{1,0:T(8,128)}, u32[]{:S(2)}, u32[]{:S(2)}) collective-permute-start(f32[512,512]{1,0:T(8,128)} %collective-permute-done.17.refs_6_), channel_id=1, source_target_pairs={{0,1},{8,11},{1,2},{9,8},{2,3},{10,9},{3,0},{11,10},{4,5},{12,15},... | collective-permute-start | bytes 3145736 | tf_op jit(solution)/shard_map/ppermute | solution.py:37
  129.7 17.4 %collective-permute-start.22 = (f32[2,2,512,128]{3,2,1,0:T(8,128)}, f32[2,2,512,128]{3,2,1,0:T(8,128)}, u32[]{:S(2)}, u32[]{:S(2)}) collective-permute-start(f32[2,2,512,128]{3,2,1,0:T(8,128)} %collective-permute-done.18.refs_4_), channel_id=1, source_target_pairs={{0,64},{8,200},{64,128},{72,8},{128,192},{136,72},{192,0},{200,136... | collective-permute-start | bytes 3145736 | tf_op jit(solution)/shard_map/ppermute | solution.py:42
  131.2 24.9 %collective-permute-start.23 = (f32[2,2,512,128]{3,2,1,0:T(8,128)}, f32[2,2,512,128]{3,2,1,0:T(8,128)}, u32[]{:S(2)}, u32[]{:S(2)}) collective-permute-start(f32[2,2,512,128]{3,2,1,0:T(8,128)} %collective-permute-done.19.refs_5_), channel_id=1, source_target_pairs={{0,64},{8,200},{64,128},{72,8},{128,192},{136,72},{192,0},{200,136... | collective-permute-start | bytes 3145736 | tf_op jit(solution)/shard_map/ppermute | solution.py:42
  132.4 23.7 %collective-permute-start.20 = (f32[512,512]{1,0:T(8,128)}, f32[512,512]{1,0:T(8,128)}, u32[]{:S(2)}, u32[]{:S(2)}) collective-permute-start(f32[512,512]{1,0:T(8,128)} %collective-permute-done.16.refs_12_.refs_14_), channel_id=1, source_target_pairs={{0,16},{8,60},{16,32},{24,8},{32,48},{40,24},{48,4},{56,40},{4,20}... | collective-permute-start | bytes 3145736 | tf_op jit(solution)/shard_map/ppermute | solution.py:32
  185.9 16.7 %collective-permute-start.28 = (f32[256,512]{1,0:T(8,128)}, f32[256,512]{1,0:T(8,128)S(1)}, u32[]{:S(2)}, u32[]{:S(2)}) collective-permute-start(f32[256,512]{1,0:T(8,128)} %get-tuple-element.89), channel_id=1, source_target_pairs={{0,8},{8,0},{1,9},{9,1},{2,10},{10,2},{3,11},{11,3},{4,12},{12,4},... | collective-permute-start | bytes 1572872 | tf_op jit(solution)/shard_map/ppermute | solution.py:46
  189.8 12.9 %collective-permute-start.27 = (f32[256,512]{1,0:T(8,128)S(1)}, f32[256,512]{1,0:T(8,128)S(1)}, u32[]{:S(2)}, u32[]{:S(2)}) collective-permute-start(f32[256,512]{1,0:T(8,128)S(1)} %add.45), channel_id=1, source_target_pairs={{0,16},{8,60},{16,32},{24,8},{32,48},{40,24},{48,4},{56,40},{4,20}... | collective-permute-start | bytes 1572872 | tf_op jit(solution)/shard_map/ppermute | solution.py:32
  189.9 13.1 %collective-permute-start.34 = (f32[256,512]{1,0:T(8,128)S(1)}, f32[256,512]{1,0:T(8,128)S(1)}, u32[]{:S(2)}, u32[]{:S(2)}) collective-permute-start(f32[256,512]{1,0:T(8,128)S(1)} %copy-done.31), channel_id=1, source_target_pairs={{0,8},{8,0},{1,9},{9,1},{2,10},{10,2},{3,11},{11,3},{4,12},{12,4},... | collective-permute-start | bytes 1572872 | tf_op jit(solution)/shard_map/ppermute | solution.py:46
  190.2 15.7 %collective-permute-start.33 = (f32[256,512]{1,0:T(8,128)S(1)}, f32[256,512]{1,0:T(8,128)S(1)}, u32[]{:S(2)}, u32[]{:S(2)}) collective-permute-start(f32[256,512]{1,0:T(8,128)S(1)} %add.46), channel_id=1, source_target_pairs={{0,16},{8,60},{16,32},{24,8},{32,48},{40,24},{48,4},{56,40},{4,20}... | collective-permute-start | bytes 1572872 | tf_op jit(solution)/shard_map/ppermute | solution.py:32
  206.1 12.9 %collective-permute-start.35 = (f32[256,512]{1,0:T(8,128)S(1)}, f32[256,512]{1,0:T(8,128)S(1)}, u32[]{:S(2)}, u32[]{:S(2)}) collective-permute-start(f32[256,512]{1,0:T(8,128)S(1)} %add_add_fusion.2), channel_id=1, source_target_pairs={{0,16},{8,60},{16,32},{24,8},{32,48},{40,24},{48,4},{56,40},{4,20}... | collective-permute-start | bytes 1572872 | tf_op jit(solution)/shard_map/ppermute | solution.py:32
  206.2 14.8 %collective-permute-start.32 = (f32[256,512]{1,0:T(8,128)S(1)}, f32[256,512]{1,0:T(8,128)S(1)}, u32[]{:S(2)}, u32[]{:S(2)}) collective-permute-start(f32[256,512]{1,0:T(8,128)S(1)} %copy-done.30), channel_id=1, source_target_pairs={{0,8},{8,0},{1,9},{9,1},{2,10},{10,2},{3,11},{11,3},{4,12},{12,4},... | collective-permute-start | bytes 1572872 | tf_op jit(solution)/shard_map/ppermute | solution.py:46
  206.3 18.5 %collective-permute-start.38 = (f32[256,512]{1,0:T(8,128)S(1)}, f32[256,512]{1,0:T(8,128)S(1)}, u32[]{:S(2)}, u32[]{:S(2)}) collective-permute-start(f32[256,512]{1,0:T(8,128)S(1)} %copy-done.29), channel_id=1, source_target_pairs={{0,8},{8,0},{1,9},{9,1},{2,10},{10,2},{3,11},{11,3},{4,12},{12,4},... | collective-permute-start | bytes 1572872 | tf_op jit(solution)/shard_map/ppermute | solution.py:46
  213.5 11.1 %collective-permute-start.31 = (f32[256,512]{1,0:T(8,128)S(1)}, f32[256,512]{1,0:T(8,128)S(1)}, u32[]{:S(2)}, u32[]{:S(2)}) collective-permute-start(f32[256,512]{1,0:T(8,128)S(1)} %add_add_fusion.4), channel_id=1, source_target_pairs={{0,16},{8,60},{16,32},{24,8},{32,48},{40,24},{48,4},{56,40},{4,20}... | collective-permute-start | bytes 1572872 | tf_op jit(solution)/shard_map/ppermute | solution.py:32
  219.2 11.1 %collective-permute-start.37 = (f32[256,512]{1,0:T(8,128)S(1)}, f32[256,512]{1,0:T(8,128)S(1)}, u32[]{:S(2)}, u32[]{:S(2)}) collective-permute-start(f32[256,512]{1,0:T(8,128)S(1)} %add_add_fusion.1), channel_id=1, source_target_pairs={{0,16},{8,60},{16,32},{24,8},{32,48},{40,24},{48,4},{56,40},{4,20}... | collective-permute-start | bytes 1572872 | tf_op jit(solution)/shard_map/ppermute | solution.py:32
  (39 other events, 698.2 us)

commit v2 on v1

--- a/solution.py
+++ b/solution.py
@@ -377,8 +377,8 @@
     )(place, mask, total)
 
 
-def from_all_y(part):
-    return [part] + [lax.ppermute(part, "y", [(y, (y + k) % NY) for y in range(NY)]) for k in range(1, NY)]
+def from_y(part, k):
+    return lax.ppermute(part, "y", [(y, (y + k) % NY) for y in range(NY)])
 
 
 def per_device(root_inverse, lower_panel, panel_mask, factor_inverse):
@@ -398,15 +398,18 @@
         ends = [ring]
         ring.append(z_step(ring[-1]))
         if r == 0:
-            pieces = from_all_y(piece)
-            ring[1], pieces[1], pieces[3] = lax.optimization_barrier((ring[1], pieces[1], pieces[3]))
+            back, ahead = from_y(piece, 1), from_y(piece, NY - 1)
+            ring[1], back, ahead = lax.optimization_barrier((ring[1], back, ahead))
         if len(ring) < NZ:
             ring.append(z_step(ring[-1]))
         if r == 0:
-            groups_of = [[jnp.stack(pieces[:2])], [jnp.stack(pieces[2:])]]
+            opposite = y_step(jnp.where(core == 0, back, ahead))
+            groups_of = [[jnp.stack([piece, back])], [jnp.stack([opposite, ahead])]]
+            groups_of[0].append(x_step(groups_of[0][0]))
         else:
             for group in groups_of:
-                group.append(x_step(group[-1]))
+                if len(group) < NX:
+                    group.append(x_step(group[-1]))
             rows = rows_near if r == 1 else rows_far
             for _ in range(min(2, NY - len(rows))):
                 rows.append(y_step(rows[-1]))

time: 232 us -> 226 us (0.974)
  waiting for transfers between devices: 132 us -> 118 us
  starting transfers between devices: 38.6 us -> 43.4 us
    ppermute x3 -> x2, waiting for transfers between devices: 29.6 us -> 14.6 us  [from_y(): return lax.ppermute(part, 'y', [(y, (y + k) % NY) for y in range(NY)])]
    ppermute x6 -> x7, waiting for transfers between devices: 30.8 us -> 41.1 us  [y_step(): return lax.ppermute(block, ('core', 'y'), pairs)]
    ppermute x6, waiting for transfers between devices: 29.9 us -> 22 us  [x_step(): return lax.ppermute(block, ('leaf', 'core'), pairs)]
    ppermute x13, starting transfers between devices: 8.66 us -> 12.2 us  [z_step(): return lax.ppermute(block, ('z_lo', 'core', 'z_hi'), pairs)]
    ppermute x11, starting transfers between devices: 10.7 us -> 14.1 us  [swap(): return lax.ppermute(block, axis, [(0, 1), (1, 0)])]
    ppermute x6 -> x7, starting transfers between devices: 7.5 us -> 8.35 us  [y_step(): return lax.ppermute(block, ('core', 'y'), pairs)]
  transfers between devices with their start and end apart: 39 -> 39, of which waited for: 23 -> 24; matrix products, arithmetic and copies ran while one was open for 2% -> 3% of each run, Pallas kernels for 11% -> 11%
where the time goes in v2:
time: 226 us; the launch traced here: 225 us
  waiting for transfers between devices  118 us (52%)
  Pallas kernels  49.5 us (22%)
  starting transfers between devices  43.4 us (19%)
  other arithmetic  7.69 us (3%)
  local copies, waits for them, and re-layouts  5.12 us (2%)
    ppermute x7, waiting for transfers between devices, y_step(): return lax.ppermute(block, ('core', 'y'), pairs)  41.1 us
    pallas_call x2, Pallas kernels, accumulate(): pl.pallas_call(functools.partial(gather_kernel, have, had), out_shape=(sh...  27.4 us
    ppermute x13, waiting for transfers between devices, z_step(): return lax.ppermute(block, ('z_lo', 'core', 'z_hi'), pairs)  27.1 us
    ppermute x6, waiting for transfers between devices, x_step(): return lax.ppermute(block, ('leaf', 'core'), pairs)  22 us
    ppermute x2, waiting for transfers between devices, from_y(): return lax.ppermute(part, 'y', [(y, (y + k) % NY) for y in range(NY)])  14.6 us
    ppermute x11, starting transfers between devices, swap(): return lax.ppermute(block, axis, [(0, 1), (1, 0)])  14.1 us
    ppermute x11, waiting for transfers between devices, swap(): return lax.ppermute(block, axis, [(0, 1), (1, 0)])  13.4 us
    ppermute x13, starting transfers between devices, z_step(): return lax.ppermute(block, ('z_lo', 'core', 'z_hi'), pairs)  12.2 us
  transfers between devices with their start and end apart: 39, of which 24 were waited for; matrix products, arithmetic and copies ran while one was open for 3% of the time, Pallas kernels for 11%

profile of v2, /device:TPU:10, one launch (start us, length us, event | category | flops | bytes accessed | tf_op | source)
XLA Modules:
  0.0 225.0 jit_solution(18099118138108716583)
XLA Ops:
  5.1 7.2 %collective-permute-start = (f32[512,128]{1,0:T(8,128)}, f32[512,128]{1,0:T(8,128)S(1)}, u32[]{:S(2)}, u32[]{:S(2)}) collective-permute-start(f32[512,128]{1,0:T(8,128)} %param.4), channel_id=1, source_target_pairs={{0,4},{4,0},{1,5},{5,1},{2,6},{6,2},{3,7},{7,3},{8,12},{12,8},{9,1... | collective-permute-start | bytes 786440 | tf_op jit(solution)/shard_map/ppermute | solution.py:46
  12.3 6.2 %collective-permute-done = f32[512,128]{1,0:T(8,128)S(1)} collective-permute-done((f32[512,128]{1,0:T(8,128)}, f32[512,128]{1,0:T(8,128)S(1)}, u32[]{:S(2)}, u32[]{:S(2)}) %collective-permute-start) | collective-permute-done | bytes 262176 | tf_op jit(solution)/shard_map/ppermute | solution.py:46
  21.2 5.7 %collective-permute-start.3 = (f32[512,512]{1,0:T(8,128)S(1)}, f32[512,512]{1,0:T(8,128)}, u32[]{:S(2)}, u32[]{:S(2)}) collective-permute-start(f32[512,512]{1,0:T(8,128)S(1)} %get-tuple-element.54.refs_6_.refs_8_), channel_id=1, source_target_pairs={{0,16},{8,60},{16,32},{24,8},{32,48},{40,24},{48,4},{56,40},{4,20}... | collective-permute-start | bytes 3145736 | tf_op jit(solution)/shard_map/ppermute | solution.py:32
  26.9 2.4 %collective-permute-start.5 = (f32[2,512,128]{2,1,0:T(8,128)S(1)}, f32[2,512,128]{2,1,0:T(8,128)S(1)}, u32[]{:S(2)}, u32[]{:S(2)}) collective-permute-start(f32[2,512,128]{2,1,0:T(8,128)S(1)} %pad_maximum_fusion.2), channel_id=1, source_target_pairs={{0,3},{1,0},{2,1},{3,2},{4,7},{5,4},{6,5},{7,6},{8,11},{9,8},{10,9... | collective-permute-start | bytes 1572872 | tf_op jit(solution)/shard_map/ppermute | solution.py:381
  29.3 12.2 %collective-permute-done.5 = f32[2,512,128]{2,1,0:T(8,128)S(1)} collective-permute-done((f32[2,512,128]{2,1,0:T(8,128)S(1)}, f32[2,512,128]{2,1,0:T(8,128)S(1)}, u32[]{:S(2)}, u32[]{:S(2)}) %collective-permute-start.5) | collective-permute-done | bytes 524320 | tf_op jit(solution)/shard_map/ppermute | solution.py:381
  41.5 2.4 %collective-permute-done.4 = f32[2,512,128]{2,1,0:T(8,128)S(1)} collective-permute-done((f32[2,512,128]{2,1,0:T(8,128)S(1)}, f32[2,512,128]{2,1,0:T(8,128)S(1)}, u32[]{:S(2)}, u32[]{:S(2)}) %collective-permute-start.4) | collective-permute-done | bytes 524320 | tf_op jit(solution)/shard_map/ppermute | solution.py:381
  46.9 9.1 %collective-permute-done.8 = f32[2,512,128]{2,1,0:T(8,128)S(1)} collective-permute-done((f32[2,512,128]{2,1,0:T(8,128)S(1)}, f32[2,512,128]{2,1,0:T(8,128)S(1)}, u32[]{:S(2)}, u32[]{:S(2)}) %collective-permute-start.8) | collective-permute-done | bytes 524320 | tf_op jit(solution)/shard_map/ppermute | solution.py:37
  57.2 1.8 collective-permute-done.7.refs_2_
  59.0 2.9 %collective-permute-done.6.refs_8_.refs_10_ = f32[512,512]{1,0:T(8,128)} collective-permute-done((f32[512,512]{1,0:T(8,128)}, f32[512,512]{1,0:T(8,128)}, u32[]{:S(2)}, u32[]{:S(2)}) %collective-permute-start.6) | collective-permute-done | bytes 1048608 | tf_op jit(solution)/shard_map/ppermute | solution.py:32
  63.8 12.9 %collective-permute-done.9.refs_2_ = f32[512,512]{1,0:T(8,128)S(1)} collective-permute-done((f32[512,512]{1,0:T(8,128)S(1)}, f32[512,512]{1,0:T(8,128)S(1)}, u32[]{:S(2)}, u32[]{:S(2)}) %collective-permute-start.9) | collective-permute-done | bytes 1048608 | tf_op jit(solution)/shard_map/ppermute | solution.py:37
  78.2 10.0 %collective-permute-done.14.refs_3_ = f32[2,2,512,128]{3,2,1,0:T(8,128)S(1)} collective-permute-done((f32[2,2,512,128]{3,2,1,0:T(8,128)S(1)}, f32[2,2,512,128]{3,2,1,0:T(8,128)S(1)}, u32[]{:S(2)}, u32[]{:S(2)}) %collective-permute-start.14) | collective-permute-done | bytes 1048608 | tf_op jit(solution)/shard_map/ppermute | solution.py:42
  88.3 4.4 %collective-permute-done.12.refs_3_ = f32[512,512]{1,0:T(8,128)S(1)} collective-permute-done((f32[512,512]{1,0:T(8,128)S(1)}, f32[512,512]{1,0:T(8,128)S(1)}, u32[]{:S(2)}, u32[]{:S(2)}) %collective-permute-start.12) | collective-permute-done | bytes 1048608 | tf_op jit(solution)/shard_map/ppermute | solution.py:37
  94.6 2.7 %collective-permute-start.15 = (f32[512,512]{1,0:T(8,128)S(1)}, f32[512,512]{1,0:T(8,128)S(1)}, u32[]{:S(2)}, u32[]{:S(2)}) collective-permute-start(f32[512,512]{1,0:T(8,128)S(1)} %shard_map.60.refs_4_), channel_id=1, source_target_pairs={{0,1},{8,11},{1,2},{9,8},{2,3},{10,9},{3,0},{11,10},{4,5},{12,15},... | collective-permute-start | bytes 3145736 | tf_op jit(solution)/shard_map/ppermute | solution.py:37
  98.9 11.5 %collective-permute-done.15.refs_5_ = f32[512,512]{1,0:T(8,128)S(1)} collective-permute-done((f32[512,512]{1,0:T(8,128)S(1)}, f32[512,512]{1,0:T(8,128)S(1)}, u32[]{:S(2)}, u32[]{:S(2)}) %collective-permute-start.15) | collective-permute-done | bytes 1048608 | tf_op jit(solution)/shard_map/ppermute | solution.py:37
  113.3 10.1 %collective-permute-done.20.refs_5_ = f32[2,2,512,128]{3,2,1,0:T(8,128)} collective-permute-done((f32[2,2,512,128]{3,2,1,0:T(8,128)S(1)}, f32[2,2,512,128]{3,2,1,0:T(8,128)}, u32[]{:S(2)}, u32[]{:S(2)}) %collective-permute-start.20) | collective-permute-done | bytes 1048608 | tf_op jit(solution)/shard_map/ppermute | solution.py:42
  123.4 3.1 %collective-permute-done.18.refs_6_ = f32[512,512]{1,0:T(8,128)} collective-permute-done((f32[512,512]{1,0:T(8,128)S(1)}, f32[512,512]{1,0:T(8,128)}, u32[]{:S(2)}, u32[]{:S(2)}) %collective-permute-start.18) | collective-permute-done | bytes 1048608 | tf_op jit(solution)/shard_map/ppermute | solution.py:37
  126.5 2.9 %collective-permute-done.17.refs_12_.refs_14_ = f32[512,512]{1,0:T(8,128)} collective-permute-done((f32[512,512]{1,0:T(8,128)S(1)}, f32[512,512]{1,0:T(8,128)}, u32[]{:S(2)}, u32[]{:S(2)}) %collective-permute-start.17) | collective-permute-done | bytes 1048608 | tf_op jit(solution)/shard_map/ppermute | solution.py:32
  129.4 2.1 collective-permute-start.22
  133.4 14.0 %shard_map.61 = (f32[2,512,512]{2,1,0:T(8,128)}, f32[2,512,512]{2,1,0:T(8,128)}) custom-call(s32[5]{0:T(128)} %stack.50.place, f32[2,2,512,128]{3,2,1,0:T(8,128)} %copy-done.9, f32[2,2,512,128]{3,2,1,0:T(8,128)} %copy-done.10, f32[2,2,512,128]{3,2,1,0:T(8,128)} %collective-permute-done.7.refs_2_, f32[2,2,512,128]{3,2,1,0:T(8,128)} %copy-done.22, ...), custom_call_target="tpu_custom_call" | custom-call | flops 4831838208 | bytes 18874368 | tf_op jit(solution)/shard_map/pallas_call | solution.py:282
  149.1 13.5 %shard_map.62 = (f32[2,512,512]{2,1,0:T(8,128)}, f32[2,512,512]{2,1,0:T(8,128)}) custom-call(s32[5]{0:T(128)} %stack.50.place, f32[2,2,512,128]{3,2,1,0:T(8,128)} %copy-done.9, f32[2,2,512,128]{3,2,1,0:T(8,128)} %copy-done.10, f32[2,2,512,128]{3,2,1,0:T(8,128)} %collective-permute-done.7.refs_2_, ...), custom_call_target="tpu_custom_call", output_to_operand_aliasing={{0}: (17, {}), {1}: (18, {})} | custom-call | flops 4831838208 | bytes 18874368 | tf_op jit(solution)/shard_map/pallas_call | solution.py:282
  162.6 4.4 %collective-permute-done.24.refs_9_ = f32[2,512,512]{2,1,0:T(8,128)S(1)} collective-permute-done((f32[2,512,512]{2,1,0:T(8,128)}, f32[2,512,512]{2,1,0:T(8,128)S(1)}, u32[]{:S(2)}, u32[]{:S(2)}) %collective-permute-start.24) | collective-permute-done | bytes 2097184 | tf_op jit(solution)/shard_map/ppermute | solution.py:46
  168.3 10.0 %shard_map.63 = (f32[2,512,512]{2,1,0:T(8,128)}, f32[256,512]{1,0:T(8,128)}, f32[256,512]{1,0:T(8,128)}, f32[256,512]{1,0:T(8,128)}, f32[256,512]{1,0:T(8,128)},...) custom-call(s32[5]{0:T(128)} %stack.50.place, f32[512,512]{1,0:T(8,128)} %copy-done.3, ...), custom_call_target="tpu_custom_call" | custom-call | flops 1610612736 | bytes 6291456 | tf_op jit(solution)/shard_map/pallas_call | solution.py:320
  183.0 3.3 %collective-permute-start.34 = (f32[256,512]{1,0:T(8,128)S(1)}, f32[256,512]{1,0:T(8,128)S(1)}, u32[]{:S(2)}, u32[]{:S(2)}) collective-permute-start(f32[256,512]{1,0:T(8,128)S(1)} %copy-done.33), channel_id=1, source_target_pairs={{0,8},{8,0},{1,9},{9,1},{2,10},{10,2},{3,11},{11,3},{4,12},{12,4},... | collective-permute-start | bytes 1572872 | tf_op jit(solution)/shard_map/ppermute | solution.py:46
  186.3 9.1 %shard_map.65 = (f32[256,512]{1,0:T(8,128)}, f32[256,512]{1,0:T(8,128)}, f32[256,512]{1,0:T(8,128)}, f32[256,512]{1,0:T(8,128)}, f32[256,512]{1,0:T(8,128)}, /*i...) custom-call(s32[5]{0:T(128)} %stack.50.place, f32[512,512]{1,0:T(8,128)} %copy-done.3, ...), custom_call_target="tpu_custom_call" | custom-call | tf_op jit(solution)/shard_map/pallas_call | solution.py:343
  196.3 2.9 %collective-permute-start.29 = (f32[256,512]{1,0:T(8,128)S(1)}, f32[256,512]{1,0:T(8,128)S(1)}, u32[]{:S(2)}, u32[]{:S(2)}) collective-permute-start(f32[256,512]{1,0:T(8,128)S(1)} %add_add_fusion.5), channel_id=1, source_target_pairs={{0,16},{8,60},{16,32},{24,8},{32,48},{40,24},{48,4},{56,40},{4,20}... | collective-permute-start | bytes 1572872 | tf_op jit(solution)/shard_map/ppermute | solution.py:32
  199.7 1.7 collective-permute-start.32
  201.5 5.3 %collective-permute-done.29 = f32[256,512]{1,0:T(8,128)S(1)} collective-permute-done((f32[256,512]{1,0:T(8,128)S(1)}, f32[256,512]{1,0:T(8,128)S(1)}, u32[]{:S(2)}, u32[]{:S(2)}) %collective-permute-start.29) | collective-permute-done | bytes 524320 | tf_op jit(solution)/shard_map/ppermute | solution.py:32
  207.0 1.7 collective-permute-start.31
  208.7 3.8 %collective-permute-done.35 = f32[256,512]{1,0:T(8,128)S(1)} collective-permute-done((f32[256,512]{1,0:T(8,128)S(1)}, f32[256,512]{1,0:T(8,128)S(1)}, u32[]{:S(2)}, u32[]{:S(2)}) %collective-permute-start.35) | collective-permute-done | bytes 524320 | tf_op jit(solution)/shard_map/ppermute | solution.py:32
  214.3 1.7 shard_map.64
  216.0 2.1 collective-permute-done.31
  218.2 5.5 %collective-permute-done.37 = f32[256,512]{1,0:T(8,128)S(1)} collective-permute-done((f32[256,512]{1,0:T(8,128)S(1)}, f32[256,512]{1,0:T(8,128)S(1)}, u32[]{:S(2)}, u32[]{:S(2)}) %collective-permute-start.37) | collective-permute-done | bytes 524320 | tf_op jit(solution)/shard_map/ppermute | solution.py:32
  (136 shorter events, 35.3 us)
Async XLA Ops:
  3.4 17.7 %collective-permute-start.2 = (f32[512,512]{1,0:T(8,128)S(1)}, f32[512,512]{1,0:T(8,128)S(1)}, u32[]{:S(2)}, u32[]{:S(2)}) collective-permute-start(f32[512,512]{1,0:T(8,128)S(1)} %get-tuple-element.52.refs_0_), channel_id=1, source_target_pairs={{0,1},{8,11},{1,2},{9,8},{2,3},{10,9},{3,0},{11,10},{4,5},{12,15},... | collective-permute-start | bytes 3145736 | tf_op jit(solution)/shard_map/ppermute | solution.py:37
  5.1 13.4 %collective-permute-start = (f32[512,128]{1,0:T(8,128)}, f32[512,128]{1,0:T(8,128)S(1)}, u32[]{:S(2)}, u32[]{:S(2)}) collective-permute-start(f32[512,128]{1,0:T(8,128)} %param.4), channel_id=1, source_target_pairs={{0,4},{4,0},{1,5},{5,1},{2,6},{6,2},{3,7},{7,3},{8,12},{12,8},{9,1... | collective-permute-start | bytes 786440 | tf_op jit(solution)/shard_map/ppermute | solution.py:46
  21.2 22.7 %collective-permute-start.3 = (f32[512,512]{1,0:T(8,128)S(1)}, f32[512,512]{1,0:T(8,128)}, u32[]{:S(2)}, u32[]{:S(2)}) collective-permute-start(f32[512,512]{1,0:T(8,128)S(1)} %get-tuple-element.54.refs_6_.refs_8_), channel_id=1, source_target_pairs={{0,16},{8,60},{16,32},{24,8},{32,48},{40,24},{48,4},{56,40},{4,20}... | collective-permute-start | bytes 3145736 | tf_op jit(solution)/shard_map/ppermute | solution.py:32
  26.9 14.6 %collective-permute-start.5 = (f32[2,512,128]{2,1,0:T(8,128)S(1)}, f32[2,512,128]{2,1,0:T(8,128)S(1)}, u32[]{:S(2)}, u32[]{:S(2)}) collective-permute-start(f32[2,512,128]{2,1,0:T(8,128)S(1)} %pad_maximum_fusion.2), channel_id=1, source_target_pairs={{0,3},{1,0},{2,1},{3,2},{4,7},{5,4},{6,5},{7,6},{8,11},{9,8},{10,9... | collective-permute-start | bytes 1572872 | tf_op jit(solution)/shard_map/ppermute | solution.py:381
  29.3 14.6 %collective-permute-start.4 = (f32[2,512,128]{2,1,0:T(8,128)S(1)}, f32[2,512,128]{2,1,0:T(8,128)S(1)}, u32[]{:S(2)}, u32[]{:S(2)}) collective-permute-start(f32[2,512,128]{2,1,0:T(8,128)S(1)} %pad_maximum_fusion.2), channel_id=1, source_target_pairs={{0,1},{1,2},{2,3},{3,0},{4,5},{5,6},{6,7},{7,4},{8,9},{9,10},{10,1... | collective-permute-start | bytes 1572872 | tf_op jit(solution)/shard_map/ppermute | solution.py:381
  44.0 15.0 %collective-permute-start.7 = (f32[2,2,512,128]{3,2,1,0:T(8,128)S(1)}, f32[2,2,512,128]{3,2,1,0:T(8,128)}, u32[]{:S(2)}, u32[]{:S(2)}) collective-permute-start(f32[2,2,512,128]{3,2,1,0:T(8,128)S(1)} %pad_maximum_fusion.refs_0_), channel_id=1, source_target_pairs={{0,64},{8,200},{64,128},{72,8},{128,192},{136,72},{192,0},{200,136... | collective-permute-start | bytes 3145736 | tf_op jit(solution)/shard_map/ppermute | solution.py:42
  45.6 16.3 %collective-permute-start.6 = (f32[512,512]{1,0:T(8,128)}, f32[512,512]{1,0:T(8,128)}, u32[]{:S(2)}, u32[]{:S(2)}) collective-permute-start(f32[512,512]{1,0:T(8,128)} %collective-permute-done.3.refs_7_.refs_9_), channel_id=1, source_target_pairs={{0,16},{8,60},{16,32},{24,8},{32,48},{40,24},{48,4},{56,40},{4,20}... | collective-permute-start | bytes 3145736 | tf_op jit(solution)/shard_map/ppermute | solution.py:32
  61.9 14.8 %collective-permute-start.9 = (f32[512,512]{1,0:T(8,128)S(1)}, f32[512,512]{1,0:T(8,128)S(1)}, u32[]{:S(2)}, u32[]{:S(2)}) collective-permute-start(f32[512,512]{1,0:T(8,128)S(1)} %copy-done.12), channel_id=1, source_target_pairs={{0,1},{8,11},{1,2},{9,8},{2,3},{10,9},{3,0},{11,10},{4,5},{12,15},... | collective-permute-start | bytes 3145736 | tf_op jit(solution)/shard_map/ppermute | solution.py:37
  62.0 16.2 %collective-permute-start.10 = (f32[512,512]{1,0:T(8,128)}, f32[512,512]{1,0:T(8,128)S(1)}, u32[]{:S(2)}, u32[]{:S(2)}) collective-permute-start(f32[512,512]{1,0:T(8,128)} %collective-permute-done.6.refs_8_.refs_10_), channel_id=1, source_target_pairs={{0,16},{8,60},{16,32},{24,8},{32,48},{40,24},{48,4},{56,40},{4,20}... | collective-permute-start | bytes 3145736 | tf_op jit(solution)/shard_map/ppermute | solution.py:32
  62.0 16.2 %collective-permute-start.13 = (f32[2,2,512,128]{3,2,1,0:T(8,128)}, f32[2,2,512,128]{3,2,1,0:T(8,128)S(1)}, u32[]{:S(2)}, u32[]{:S(2)}) collective-permute-start(f32[2,2,512,128]{3,2,1,0:T(8,128)} %collective-permute-done.7.refs_2_), channel_id=1, source_target_pairs={{0,64},{8,200},{64,128},{72,8},{128,192},{136,72},{192,0},{200,136... | collective-permute-start | bytes 3145736 | tf_op jit(solution)/shard_map/ppermute | solution.py:42
  63.2 25.0 %collective-permute-start.14 = (f32[2,2,512,128]{3,2,1,0:T(8,128)S(1)}, f32[2,2,512,128]{3,2,1,0:T(8,128)S(1)}, u32[]{:S(2)}, u32[]{:S(2)}) collective-permute-start(f32[2,2,512,128]{3,2,1,0:T(8,128)S(1)} %pad_maximum_fusion.1.refs_1_), channel_id=1, source_target_pairs={{0,64},{8,200},{64,128},{72,8},{128,192},{136,72},{192,0},{200,136... | collective-permute-start | bytes 3145736 | tf_op jit(solution)/shard_map/ppermute | solution.py:42
  76.7 16.0 %collective-permute-start.12 = (f32[512,512]{1,0:T(8,128)S(1)}, f32[512,512]{1,0:T(8,128)S(1)}, u32[]{:S(2)}, u32[]{:S(2)}) collective-permute-start(f32[512,512]{1,0:T(8,128)S(1)} %collective-permute-done.9.refs_2_), channel_id=1, source_target_pairs={{0,1},{8,11},{1,2},{9,8},{2,3},{10,9},{3,0},{11,10},{4,5},{12,15},... | collective-permute-start | bytes 3145736 | tf_op jit(solution)/shard_map/ppermute | solution.py:37
  78.2 16.0 %collective-permute-start.11 = (f32[512,512]{1,0:T(8,128)S(1)}, f32[512,512]{1,0:T(8,128)S(1)}, u32[]{:S(2)}, u32[]{:S(2)}) collective-permute-start(f32[512,512]{1,0:T(8,128)S(1)} %collective-permute-done.10.refs_9_.refs_11_), channel_id=1, source_target_pairs={{0,16},{8,60},{16,32},{24,8},{32,48},{40,24},{48,4},{56,40},{4,20}... | collective-permute-start | bytes 3145736 | tf_op jit(solution)/shard_map/ppermute | solution.py:32
  94.6 15.8 %collective-permute-start.15 = (f32[512,512]{1,0:T(8,128)S(1)}, f32[512,512]{1,0:T(8,128)S(1)}, u32[]{:S(2)}, u32[]{:S(2)}) collective-permute-start(f32[512,512]{1,0:T(8,128)S(1)} %shard_map.60.refs_4_), channel_id=1, source_target_pairs={{0,1},{8,11},{1,2},{9,8},{2,3},{10,9},{3,0},{11,10},{4,5},{12,15},... | collective-permute-start | bytes 3145736 | tf_op jit(solution)/shard_map/ppermute | solution.py:37
  97.2 16.0 %collective-permute-start.16 = (f32[512,512]{1,0:T(8,128)S(1)}, f32[512,512]{1,0:T(8,128)S(1)}, u32[]{:S(2)}, u32[]{:S(2)}) collective-permute-start(f32[512,512]{1,0:T(8,128)S(1)} %collective-permute-done.11.block.refs_10_.refs_12_), channel_id=1, source_target_pairs={{0,16},{8,60},{16,32},{24,8},{32,48},{40,24},{48,4},{56,40},{4,20}... | collective-permute-start | bytes 3145736 | tf_op jit(solution)/shard_map/ppermute | solution.py:32
  97.2 16.0 %collective-permute-start.19 = (f32[2,2,512,128]{3,2,1,0:T(8,128)S(1)}, f32[2,2,512,128]{3,2,1,0:T(8,128)S(1)}, u32[]{:S(2)}, u32[]{:S(2)}) collective-permute-start(f32[2,2,512,128]{3,2,1,0:T(8,128)S(1)} %collective-permute-done.13.refs_4_), channel_id=1, source_target_pairs={{0,64},{8,200},{64,128},{72,8},{128,192},{136,72},{192,0},{200,136... | collective-permute-start | bytes 3145736 | tf_op jit(solution)/shard_map/ppermute | solution.py:42
  98.4 24.9 %collective-permute-start.20 = (f32[2,2,512,128]{3,2,1,0:T(8,128)S(1)}, f32[2,2,512,128]{3,2,1,0:T(8,128)}, u32[]{:S(2)}, u32[]{:S(2)}) collective-permute-start(f32[2,2,512,128]{3,2,1,0:T(8,128)S(1)} %collective-permute-done.14.refs_3_), channel_id=1, source_target_pairs={{0,64},{8,200},{64,128},{72,8},{128,192},{136,72},{192,0},{200,136... | collective-permute-start | bytes 3145736 | tf_op jit(solution)/shard_map/ppermute | solution.py:42
  110.4 16.1 %collective-permute-start.18 = (f32[512,512]{1,0:T(8,128)S(1)}, f32[512,512]{1,0:T(8,128)}, u32[]{:S(2)}, u32[]{:S(2)}) collective-permute-start(f32[512,512]{1,0:T(8,128)S(1)} %collective-permute-done.15.refs_5_), channel_id=1, source_target_pairs={{0,1},{8,11},{1,2},{9,8},{2,3},{10,9},{3,0},{11,10},{4,5},{12,15},... | collective-permute-start | bytes 3145736 | tf_op jit(solution)/shard_map/ppermute | solution.py:37
  113.3 16.1 %collective-permute-start.17 = (f32[512,512]{1,0:T(8,128)S(1)}, f32[512,512]{1,0:T(8,128)}, u32[]{:S(2)}, u32[]{:S(2)}) collective-permute-start(f32[512,512]{1,0:T(8,128)S(1)} %collective-permute-done.16.refs_11_.refs_13_), channel_id=1, source_target_pairs={{0,16},{8,60},{16,32},{24,8},{32,48},{40,24},{48,4},{56,40},{4,20}... | collective-permute-start | bytes 3145736 | tf_op jit(solution)/shard_map/ppermute | solution.py:32
  129.4 18.0 %collective-permute-start.22 = (f32[512,512]{1,0:T(8,128)}, f32[512,512]{1,0:T(8,128)}, u32[]{:S(2)}, u32[]{:S(2)}) collective-permute-start(f32[512,512]{1,0:T(8,128)} %collective-permute-done.18.refs_6_), channel_id=1, source_target_pairs={{0,1},{8,11},{1,2},{9,8},{2,3},{10,9},{3,0},{11,10},{4,5},{12,15},... | collective-permute-start | bytes 3145736 | tf_op jit(solution)/shard_map/ppermute | solution.py:37
  131.5 15.9 %collective-permute-start.23 = (f32[2,2,512,128]{3,2,1,0:T(8,128)}, f32[2,2,512,128]{3,2,1,0:T(8,128)}, u32[]{:S(2)}, u32[]{:S(2)}) collective-permute-start(f32[2,2,512,128]{3,2,1,0:T(8,128)} %collective-permute-done.20.refs_5_), channel_id=1, source_target_pairs={{0,64},{8,200},{64,128},{72,8},{128,192},{136,72},{192,0},{200,136... | collective-permute-start | bytes 3145736 | tf_op jit(solution)/shard_map/ppermute | solution.py:42
  132.7 16.3 %collective-permute-start.21 = (f32[512,512]{1,0:T(8,128)}, f32[512,512]{1,0:T(8,128)}, u32[]{:S(2)}, u32[]{:S(2)}) collective-permute-start(f32[512,512]{1,0:T(8,128)} %collective-permute-done.17.refs_12_.refs_14_), channel_id=1, source_target_pairs={{0,16},{8,60},{16,32},{24,8},{32,48},{40,24},{48,4},{56,40},{4,20}... | collective-permute-start | bytes 3145736 | tf_op jit(solution)/shard_map/ppermute | solution.py:32
  179.0 17.1 %collective-permute-start.28 = (f32[256,512]{1,0:T(8,128)}, f32[256,512]{1,0:T(8,128)S(1)}, u32[]{:S(2)}, u32[]{:S(2)}) collective-permute-start(f32[256,512]{1,0:T(8,128)} %get-tuple-element.89), channel_id=1, source_target_pairs={{0,8},{8,0},{1,9},{9,1},{2,10},{10,2},{3,11},{11,3},{4,12},{12,4},... | collective-permute-start | bytes 1572872 | tf_op jit(solution)/shard_map/ppermute | solution.py:46
  182.9 13.3 %collective-permute-start.27 = (f32[256,512]{1,0:T(8,128)S(1)}, f32[256,512]{1,0:T(8,128)S(1)}, u32[]{:S(2)}, u32[]{:S(2)}) collective-permute-start(f32[256,512]{1,0:T(8,128)S(1)} %add.45), channel_id=1, source_target_pairs={{0,16},{8,60},{16,32},{24,8},{32,48},{40,24},{48,4},{56,40},{4,20}... | collective-permute-start | bytes 1572872 | tf_op jit(solution)/shard_map/ppermute | solution.py:32
  183.0 16.3 %collective-permute-start.34 = (f32[256,512]{1,0:T(8,128)S(1)}, f32[256,512]{1,0:T(8,128)S(1)}, u32[]{:S(2)}, u32[]{:S(2)}) collective-permute-start(f32[256,512]{1,0:T(8,128)S(1)} %copy-done.33), channel_id=1, source_target_pairs={{0,8},{8,0},{1,9},{9,1},{2,10},{10,2},{3,11},{11,3},{4,12},{12,4},... | collective-permute-start | bytes 1572872 | tf_op jit(solution)/shard_map/ppermute | solution.py:46
  186.3 12.9 %collective-permute-start.33 = (f32[256,512]{1,0:T(8,128)S(1)}, f32[256,512]{1,0:T(8,128)S(1)}, u32[]{:S(2)}, u32[]{:S(2)}) collective-permute-start(f32[256,512]{1,0:T(8,128)S(1)} %add.46), channel_id=1, source_target_pairs={{0,16},{8,60},{16,32},{24,8},{32,48},{40,24},{48,4},{56,40},{4,20}... | collective-permute-start | bytes 1572872 | tf_op jit(solution)/shard_map/ppermute | solution.py:32
  196.1 12.6 %collective-permute-start.36 = (f32[256,512]{1,0:T(8,128)}, f32[256,512]{1,0:T(8,128)S(1)}, u32[]{:S(2)}, u32[]{:S(2)}) collective-permute-start(f32[256,512]{1,0:T(8,128)} %get-tuple-element.99), channel_id=1, source_target_pairs={{0,8},{8,0},{1,9},{9,1},{2,10},{10,2},{3,11},{11,3},{4,12},{12,4},... | collective-permute-start | bytes 1572872 | tf_op jit(solution)/shard_map/ppermute | solution.py:46
  199.4 13.0 %collective-permute-start.35 = (f32[256,512]{1,0:T(8,128)S(1)}, f32[256,512]{1,0:T(8,128)S(1)}, u32[]{:S(2)}, u32[]{:S(2)}) collective-permute-start(f32[256,512]{1,0:T(8,128)S(1)} %add_add_fusion.2), channel_id=1, source_target_pairs={{0,16},{8,60},{16,32},{24,8},{32,48},{40,24},{48,4},{56,40},{4,20}... | collective-permute-start | bytes 1572872 | tf_op jit(solution)/shard_map/ppermute | solution.py:32
  199.7 16.3 %collective-permute-start.32 = (f32[256,512]{1,0:T(8,128)S(1)}, f32[256,512]{1,0:T(8,128)S(1)}, u32[]{:S(2)}, u32[]{:S(2)}) collective-permute-start(f32[256,512]{1,0:T(8,128)S(1)} %copy-done.32), channel_id=1, source_target_pairs={{0,8},{8,0},{1,9},{9,1},{2,10},{10,2},{3,11},{11,3},{4,12},{12,4},... | collective-permute-start | bytes 1572872 | tf_op jit(solution)/shard_map/ppermute | solution.py:46
  201.4 16.8 %collective-permute-start.38 = (f32[256,512]{1,0:T(8,128)S(1)}, f32[256,512]{1,0:T(8,128)S(1)}, u32[]{:S(2)}, u32[]{:S(2)}) collective-permute-start(f32[256,512]{1,0:T(8,128)S(1)} %copy-done.31), channel_id=1, source_target_pairs={{0,8},{8,0},{1,9},{9,1},{2,10},{10,2},{3,11},{11,3},{4,12},{12,4},... | collective-permute-start | bytes 1572872 | tf_op jit(solution)/shard_map/ppermute | solution.py:46
  207.0 11.1 %collective-permute-start.31 = (f32[256,512]{1,0:T(8,128)S(1)}, f32[256,512]{1,0:T(8,128)S(1)}, u32[]{:S(2)}, u32[]{:S(2)}) collective-permute-start(f32[256,512]{1,0:T(8,128)S(1)} %add_add_fusion.4), channel_id=1, source_target_pairs={{0,16},{8,60},{16,32},{24,8},{32,48},{40,24},{48,4},{56,40},{4,20}... | collective-permute-start | bytes 1572872 | tf_op jit(solution)/shard_map/ppermute | solution.py:32
  212.6 11.1 %collective-permute-start.37 = (f32[256,512]{1,0:T(8,128)S(1)}, f32[256,512]{1,0:T(8,128)S(1)}, u32[]{:S(2)}, u32[]{:S(2)}) collective-permute-start(f32[256,512]{1,0:T(8,128)S(1)} %add_add_fusion.1), channel_id=1, source_target_pairs={{0,16},{8,60},{16,32},{24,8},{32,48},{40,24},{48,4},{56,40},{4,20}... | collective-permute-start | bytes 1572872 | tf_op jit(solution)/shard_map/ppermute | solution.py:32
  (41 other events, 626.0 us)

commit v3 on v2

--- a/solution.py
+++ b/solution.py
@@ -416,9 +416,10 @@
             ends.append(rows)
         ends += groups_of + ([rows_near] if r == 0 else [])
         values = [into[-1] for into in ends]
-        if r == NX - 1:
-            had = (NX - 1, NZ - 1)
-            totals = accumulate(place, had, (0, 0), list(zip(*groups_of)), ring, totals)
+        if r >= 2:
+            have = (r, 2 * r + 1)
+            totals = accumulate(place, have, had, list(zip(*groups_of)), ring, totals)
+            had = have
             totals, values = lax.optimization_barrier((totals, values))
         else:
             values = lax.optimization_barrier(values)

time: 226 us -> 240 us (1.062); the launches traced: 225 us -> 235 us
  Pallas kernels: 49.5 us -> 55.3 us
    ppermute x6, waiting for transfers between devices: 22 us -> 14.1 us  [x_step(): return lax.ppermute(block, ('leaf', 'core'), pairs)]
    ppermute x13, waiting for transfers between devices: 27.1 us -> 34.8 us  [z_step(): return lax.ppermute(block, ('z_lo', 'core', 'z_hi'), pairs)]
    ppermute x11, starting transfers between devices: 14.1 us -> 20.2 us  [swap(): return lax.ppermute(block, axis, [(0, 1), (1, 0)])]
    pallas_call x2 -> x3, Pallas kernels: 27.4 us -> 33.3 us  [accumulate(): pl.pallas_call(functools.partial(gather_kernel, have, had), out_shape=(sh...]
    ppermute x13, starting transfers between devices: 12.2 us -> 7.79 us  [z_step(): return lax.ppermute(block, ('z_lo', 'core', 'z_hi'), pairs)]
    unnamed x68 -> x64, local copies, waits for them, and re-layouts: 4.46 us -> 5.41 us
  transfers between devices with their start and end apart: 39 -> 39, of which waited for: 24 -> 26; matrix products, arithmetic and copies ran while one was open for 3% -> 3% of each run, Pallas kernels for 11% -> 13%
where the time goes in v3:
time: 240 us; the launch traced here: 235 us
  waiting for transfers between devices  120 us (50%)
  Pallas kernels  55.3 us (23%)
  starting transfers between devices  45.1 us (19%)
  other arithmetic  7.69 us (3%)
  local copies, waits for them, and re-layouts  6.08 us (3%)
    ppermute x7, waiting for transfers between devices, y_step(): return lax.ppermute(block, ('core', 'y'), pairs)  42.5 us
    ppermute x13, waiting for transfers between devices, z_step(): return lax.ppermute(block, ('z_lo', 'core', 'z_hi'), pairs)  34.8 us
    pallas_call x3, Pallas kernels, accumulate(): pl.pallas_call(functools.partial(gather_kernel, have, had), out_shape=(sh...  33.3 us
    ppermute x11, starting transfers between devices, swap(): return lax.ppermute(block, axis, [(0, 1), (1, 0)])  20.2 us
    ppermute x2, waiting for transfers between devices, from_y(): return lax.ppermute(part, 'y', [(y, (y + k) % NY) for y in range(NY)])  14.6 us
    ppermute x6, waiting for transfers between devices, x_step(): return lax.ppermute(block, ('leaf', 'core'), pairs)  14.1 us
    ppermute x11, waiting for transfers between devices, swap(): return lax.ppermute(block, axis, [(0, 1), (1, 0)])  13.6 us
    pallas_call x1, Pallas kernels, first_pairs(): pl.pallas_call(body, out_shape=(shaped(2, n, n),) + (shaped(n // 2, n),)...  10 us
  transfers between devices with their start and end apart: 39, of which 26 were waited for; matrix products, arithmetic and copies ran while one was open for 3% of the time, Pallas kernels for 13%

profile of v3, /device:TPU:10, one launch (start us, length us, event | category | flops | bytes accessed | tf_op | source)
XLA Modules:
  0.0 235.1 jit_solution(8646019426641531193)
XLA Ops:
  5.1 7.2 %collective-permute-start = (f32[512,128]{1,0:T(8,128)}, f32[512,128]{1,0:T(8,128)S(1)}, u32[]{:S(2)}, u32[]{:S(2)}) collective-permute-start(f32[512,128]{1,0:T(8,128)} %param.4), channel_id=1, source_target_pairs={{0,4},{4,0},{1,5},{5,1},{2,6},{6,2},{3,7},{7,3},{8,12},{12,8},{9,1... | collective-permute-start | bytes 786440 | tf_op jit(solution)/shard_map/ppermute | solution.py:46
  12.3 6.2 %collective-permute-done = f32[512,128]{1,0:T(8,128)S(1)} collective-permute-done((f32[512,128]{1,0:T(8,128)}, f32[512,128]{1,0:T(8,128)S(1)}, u32[]{:S(2)}, u32[]{:S(2)}) %collective-permute-start) | collective-permute-done | bytes 262176 | tf_op jit(solution)/shard_map/ppermute | solution.py:46
  21.2 5.7 %collective-permute-start.3 = (f32[512,512]{1,0:T(8,128)S(1)}, f32[512,512]{1,0:T(8,128)}, u32[]{:S(2)}, u32[]{:S(2)}) collective-permute-start(f32[512,512]{1,0:T(8,128)S(1)} %get-tuple-element.58.refs_4_.refs_6_.refs_8_), channel_id=1, source_target_pairs={{0,16},{8,60},{16,32},{24,8},{32,48},{40,24},{48,4},{56,40},{4,20}... | collective-permute-start | bytes 3145736 | tf_op jit(solution)/shard_map/ppermute | solution.py:32
  26.9 2.4 %collective-permute-start.5 = (f32[2,512,128]{2,1,0:T(8,128)S(1)}, f32[2,512,128]{2,1,0:T(8,128)S(1)}, u32[]{:S(2)}, u32[]{:S(2)}) collective-permute-start(f32[2,512,128]{2,1,0:T(8,128)S(1)} %pad_maximum_fusion.2), channel_id=1, source_target_pairs={{0,3},{1,0},{2,1},{3,2},{4,7},{5,4},{6,5},{7,6},{8,11},{9,8},{10,9... | collective-permute-start | bytes 1572872 | tf_op jit(solution)/shard_map/ppermute | solution.py:381
  29.3 12.2 %collective-permute-done.5 = f32[2,512,128]{2,1,0:T(8,128)S(1)} collective-permute-done((f32[2,512,128]{2,1,0:T(8,128)S(1)}, f32[2,512,128]{2,1,0:T(8,128)S(1)}, u32[]{:S(2)}, u32[]{:S(2)}) %collective-permute-start.5) | collective-permute-done | bytes 524320 | tf_op jit(solution)/shard_map/ppermute | solution.py:381
  41.5 2.4 %collective-permute-done.4 = f32[2,512,128]{2,1,0:T(8,128)S(1)} collective-permute-done((f32[2,512,128]{2,1,0:T(8,128)S(1)}, f32[2,512,128]{2,1,0:T(8,128)S(1)}, u32[]{:S(2)}, u32[]{:S(2)}) %collective-permute-start.4) | collective-permute-done | bytes 524320 | tf_op jit(solution)/shard_map/ppermute | solution.py:381
  46.9 9.1 %collective-permute-done.8 = f32[2,512,128]{2,1,0:T(8,128)S(1)} collective-permute-done((f32[2,512,128]{2,1,0:T(8,128)S(1)}, f32[2,512,128]{2,1,0:T(8,128)S(1)}, u32[]{:S(2)}, u32[]{:S(2)}) %collective-permute-start.8) | collective-permute-done | bytes 524320 | tf_op jit(solution)/shard_map/ppermute | solution.py:37
  57.2 1.8 collective-permute-done.7.refs_2_
  59.0 2.9 %collective-permute-done.6.refs_6_.refs_8_.refs_10_ = f32[512,512]{1,0:T(8,128)} collective-permute-done((f32[512,512]{1,0:T(8,128)}, f32[512,512]{1,0:T(8,128)}, u32[]{:S(2)}, u32[]{:S(2)}) %collective-permute-start.6) | collective-permute-done | bytes 1048608 | tf_op jit(solution)/shard_map/ppermute | solution.py:32
  63.8 12.9 %collective-permute-done.9.refs_2_ = f32[512,512]{1,0:T(8,128)S(1)} collective-permute-done((f32[512,512]{1,0:T(8,128)S(1)}, f32[512,512]{1,0:T(8,128)S(1)}, u32[]{:S(2)}, u32[]{:S(2)}) %collective-permute-start.9) | collective-permute-done | bytes 1048608 | tf_op jit(solution)/shard_map/ppermute | solution.py:37
  78.2 10.2 %collective-permute-done.14.refs_3_ = f32[2,2,512,128]{3,2,1,0:T(8,128)} collective-permute-done((f32[2,2,512,128]{3,2,1,0:T(8,128)S(1)}, f32[2,2,512,128]{3,2,1,0:T(8,128)}, u32[]{:S(2)}, u32[]{:S(2)}) %collective-permute-start.14) | collective-permute-done | bytes 1048608 | tf_op jit(solution)/shard_map/ppermute | solution.py:42
  88.4 4.3 %collective-permute-done.12.refs_3_ = f32[512,512]{1,0:T(8,128)S(1)} collective-permute-done((f32[512,512]{1,0:T(8,128)S(1)}, f32[512,512]{1,0:T(8,128)S(1)}, u32[]{:S(2)}, u32[]{:S(2)}) %collective-permute-start.12) | collective-permute-done | bytes 1048608 | tf_op jit(solution)/shard_map/ppermute | solution.py:37
  94.6 2.7 %collective-permute-start.15 = (f32[512,512]{1,0:T(8,128)S(1)}, f32[512,512]{1,0:T(8,128)}, u32[]{:S(2)}, u32[]{:S(2)}) collective-permute-start(f32[512,512]{1,0:T(8,128)S(1)} %shard_map.60.refs_4_), channel_id=1, source_target_pairs={{0,1},{8,11},{1,2},{9,8},{2,3},{10,9},{3,0},{11,10},{4,5},{12,15},... | collective-permute-start | bytes 3145736 | tf_op jit(solution)/shard_map/ppermute | solution.py:37
  99.0 11.6 %collective-permute-done.15.refs_5_ = f32[512,512]{1,0:T(8,128)} collective-permute-done((f32[512,512]{1,0:T(8,128)S(1)}, f32[512,512]{1,0:T(8,128)}, u32[]{:S(2)}, u32[]{:S(2)}) %collective-permute-start.15) | collective-permute-done | bytes 1048608 | tf_op jit(solution)/shard_map/ppermute | solution.py:37
  114.1 10.2 %shard_map.61 = (f32[2,512,512]{2,1,0:T(8,128)}, f32[2,512,512]{2,1,0:T(8,128)}) custom-call(s32[5]{0:T(128)} %stack.50.place, f32[2,2,512,128]{3,2,1,0:T(8,128)} %copy-done.9, f32[2,2,512,128]{3,2,1,0:T(8,128)} %copy-done.10, f32[2,2,512,128]{3,2,1,0:T(8,128)} %collective-permute-done.7.refs_2_, f32[2,2,512,128]{3,2,1,0:T(8,128)} %collective-permute-done.14.refs_3_, ...), custom_call_target="tpu_custom_call" | custom-call | flops 4831838208 | bytes 18874368 | tf_op jit(solution)/shard_map/pallas_call | solution.py:282
  124.4 2.5 %collective-permute-done.18.refs_6_ = f32[512,512]{1,0:T(8,128)} collective-permute-done((f32[512,512]{1,0:T(8,128)}, f32[512,512]{1,0:T(8,128)}, u32[]{:S(2)}, u32[]{:S(2)}) %collective-permute-start.18) | collective-permute-done | bytes 1048608 | tf_op jit(solution)/shard_map/ppermute | solution.py:37
  126.9 2.8 %collective-permute-done.17.refs_12_.refs_14_ = f32[512,512]{1,0:T(8,128)} collective-permute-done((f32[512,512]{1,0:T(8,128)}, f32[512,512]{1,0:T(8,128)}, u32[]{:S(2)}, u32[]{:S(2)}) %collective-permute-start.17) | collective-permute-done | bytes 1048608 | tf_op jit(solution)/shard_map/ppermute | solution.py:32
  129.8 2.2 collective-permute-start.22
  133.1 9.7 %shard_map.62 = (f32[2,512,512]{2,1,0:T(8,128)}, f32[2,512,512]{2,1,0:T(8,128)}) custom-call(s32[5]{0:T(128)} %stack.50.place, f32[2,2,512,128]{3,2,1,0:T(8,128)} %copy-done.9, f32[2,2,512,128]{3,2,1,0:T(8,128)} %copy-done.10, f32[2,2,512,128]{3,2,1,0:T(8,128)} %collective-permute-done.7.refs_2_, ...), custom_call_target="tpu_custom_call", output_to_operand_aliasing={{0}: (14, {}), {1}: (15, {})} | custom-call | flops 4831838208 | bytes 18874368 | tf_op jit(solution)/shard_map/pallas_call | solution.py:282
  142.8 2.0 collective-permute-done.22.refs_7_
  144.8 2.2 collective-permute-done.23.refs_7_
  146.9 2.4 %collective-permute-done.21.refs_15_ = f32[512,512]{1,0:T(8,128)S(1)} collective-permute-done((f32[512,512]{1,0:T(8,128)}, f32[512,512]{1,0:T(8,128)S(1)}, u32[]{:S(2)}, u32[]{:S(2)}) %collective-permute-start.21) | collective-permute-done | bytes 1048608 | tf_op jit(solution)/shard_map/ppermute | solution.py:32
  150.3 13.4 %shard_map.63 = (f32[2,512,512]{2,1,0:T(8,128)}, f32[2,512,512]{2,1,0:T(8,128)}) custom-call(s32[5]{0:T(128)} %stack.50.place, f32[2,2,512,128]{3,2,1,0:T(8,128)} %copy-done.9, f32[2,2,512,128]{3,2,1,0:T(8,128)} %copy-done.10, f32[2,2,512,128]{3,2,1,0:T(8,128)} %collective-permute-done.7.refs_2_, ...), custom_call_target="tpu_custom_call", output_to_operand_aliasing={{0}: (17, {}), {1}: (18, {})} | custom-call | flops 4831838208 | bytes 18874368 | tf_op jit(solution)/shard_map/pallas_call | solution.py:282
  163.7 9.3 %collective-permute-start.24 = (f32[2,512,512]{2,1,0:T(8,128)}, f32[2,512,512]{2,1,0:T(8,128)S(1)}, u32[]{:S(2)}, u32[]{:S(2)}) collective-permute-start(f32[2,512,512]{2,1,0:T(8,128)} %get-tuple-element.89), channel_id=1, source_target_pairs={{0,8},{8,0},{1,9},{9,1},{2,10},{10,2},{3,11},{11,3},{4,12},{12,4},... | collective-permute-start | bytes 6291464 | tf_op jit(solution)/shard_map/ppermute | solution.py:46
  173.0 4.4 %collective-permute-done.24.refs_9_ = f32[2,512,512]{2,1,0:T(8,128)S(1)} collective-permute-done((f32[2,512,512]{2,1,0:T(8,128)}, f32[2,512,512]{2,1,0:T(8,128)S(1)}, u32[]{:S(2)}, u32[]{:S(2)}) %collective-permute-start.24) | collective-permute-done | bytes 2097184 | tf_op jit(solution)/shard_map/ppermute | solution.py:46
  178.7 10.0 %shard_map.64 = (f32[2,512,512]{2,1,0:T(8,128)}, f32[256,512]{1,0:T(8,128)}, f32[256,512]{1,0:T(8,128)}, f32[256,512]{1,0:T(8,128)}, f32[256,512]{1,0:T(8,128)},...) custom-call(s32[5]{0:T(128)} %stack.50.place, f32[512,512]{1,0:T(8,128)} %copy-done.3, ...), custom_call_target="tpu_custom_call" | custom-call | flops 1610612736 | bytes 6291456 | tf_op jit(solution)/shard_map/pallas_call | solution.py:320
  195.2 9.1 %shard_map.66 = (f32[256,512]{1,0:T(8,128)}, f32[256,512]{1,0:T(8,128)}, f32[256,512]{1,0:T(8,128)}, f32[256,512]{1,0:T(8,128)}, f32[256,512]{1,0:T(8,128)}, /*i...) custom-call(s32[5]{0:T(128)} %stack.50.place, f32[512,512]{1,0:T(8,128)} %copy-done.3, ...), custom_call_target="tpu_custom_call" | custom-call | tf_op jit(solution)/shard_map/pallas_call | solution.py:343
  206.8 2.5 %collective-permute-done.33 = f32[256,512]{1,0:T(8,128)S(1)} collective-permute-done((f32[256,512]{1,0:T(8,128)S(1)}, f32[256,512]{1,0:T(8,128)S(1)}, u32[]{:S(2)}, u32[]{:S(2)}) %collective-permute-start.33) | collective-permute-done | bytes 524320 | tf_op jit(solution)/shard_map/ppermute | solution.py:32
  210.2 6.6 %collective-permute-done.29 = f32[256,512]{1,0:T(8,128)S(1)} collective-permute-done((f32[256,512]{1,0:T(8,128)S(1)}, f32[256,512]{1,0:T(8,128)S(1)}, u32[]{:S(2)}, u32[]{:S(2)}) %collective-permute-start.29) | collective-permute-done | bytes 524320 | tf_op jit(solution)/shard_map/ppermute | solution.py:32
  217.0 5.3 %collective-permute-done.35 = f32[256,512]{1,0:T(8,128)S(1)} collective-permute-done((f32[256,512]{1,0:T(8,128)S(1)}, f32[256,512]{1,0:T(8,128)S(1)}, u32[]{:S(2)}, u32[]{:S(2)}) %collective-permute-start.35) | collective-permute-done | bytes 524320 | tf_op jit(solution)/shard_map/ppermute | solution.py:32
  224.4 3.6 %collective-permute-done.31 = f32[256,512]{1,0:T(8,128)S(1)} collective-permute-done((f32[256,512]{1,0:T(8,128)S(1)}, f32[256,512]{1,0:T(8,128)S(1)}, u32[]{:S(2)}, u32[]{:S(2)}) %collective-permute-start.31) | collective-permute-done | bytes 524320 | tf_op jit(solution)/shard_map/ppermute | solution.py:32
  228.2 5.5 %collective-permute-done.37 = f32[256,512]{1,0:T(8,128)S(1)} collective-permute-done((f32[256,512]{1,0:T(8,128)S(1)}, f32[256,512]{1,0:T(8,128)S(1)}, u32[]{:S(2)}, u32[]{:S(2)}) %collective-permute-start.37) | collective-permute-done | bytes 524320 | tf_op jit(solution)/shard_map/ppermute | solution.py:32
  (133 shorter events, 38.4 us)
Async XLA Ops:
  3.4 17.7 %collective-permute-start.2 = (f32[512,512]{1,0:T(8,128)S(1)}, f32[512,512]{1,0:T(8,128)S(1)}, u32[]{:S(2)}, u32[]{:S(2)}) collective-permute-start(f32[512,512]{1,0:T(8,128)S(1)} %get-tuple-element.56.refs_0_), channel_id=1, source_target_pairs={{0,1},{8,11},{1,2},{9,8},{2,3},{10,9},{3,0},{11,10},{4,5},{12,15},... | collective-permute-start | bytes 3145736 | tf_op jit(solution)/shard_map/ppermute | solution.py:37
  5.1 13.4 %collective-permute-start = (f32[512,128]{1,0:T(8,128)}, f32[512,128]{1,0:T(8,128)S(1)}, u32[]{:S(2)}, u32[]{:S(2)}) collective-permute-start(f32[512,128]{1,0:T(8,128)} %param.4), channel_id=1, source_target_pairs={{0,4},{4,0},{1,5},{5,1},{2,6},{6,2},{3,7},{7,3},{8,12},{12,8},{9,1... | collective-permute-start | bytes 786440 | tf_op jit(solution)/shard_map/ppermute | solution.py:46
  21.2 22.7 %collective-permute-start.3 = (f32[512,512]{1,0:T(8,128)S(1)}, f32[512,512]{1,0:T(8,128)}, u32[]{:S(2)}, u32[]{:S(2)}) collective-permute-start(f32[512,512]{1,0:T(8,128)S(1)} %get-tuple-element.58.refs_4_.refs_6_.refs_8_), channel_id=1, source_target_pairs={{0,16},{8,60},{16,32},{24,8},{32,48},{40,24},{48,4},{56,40},{4,20}... | collective-permute-start | bytes 3145736 | tf_op jit(solution)/shard_map/ppermute | solution.py:32
  26.9 14.6 %collective-permute-start.5 = (f32[2,512,128]{2,1,0:T(8,128)S(1)}, f32[2,512,128]{2,1,0:T(8,128)S(1)}, u32[]{:S(2)}, u32[]{:S(2)}) collective-permute-start(f32[2,512,128]{2,1,0:T(8,128)S(1)} %pad_maximum_fusion.2), channel_id=1, source_target_pairs={{0,3},{1,0},{2,1},{3,2},{4,7},{5,4},{6,5},{7,6},{8,11},{9,8},{10,9... | collective-permute-start | bytes 1572872 | tf_op jit(solution)/shard_map/ppermute | solution.py:381
  29.3 14.6 %collective-permute-start.4 = (f32[2,512,128]{2,1,0:T(8,128)S(1)}, f32[2,512,128]{2,1,0:T(8,128)S(1)}, u32[]{:S(2)}, u32[]{:S(2)}) collective-permute-start(f32[2,512,128]{2,1,0:T(8,128)S(1)} %pad_maximum_fusion.2), channel_id=1, source_target_pairs={{0,1},{1,2},{2,3},{3,0},{4,5},{5,6},{6,7},{7,4},{8,9},{9,10},{10,1... | collective-permute-start | bytes 1572872 | tf_op jit(solution)/shard_map/ppermute | solution.py:381
  44.0 15.0 %collective-permute-start.7 = (f32[2,2,512,128]{3,2,1,0:T(8,128)S(1)}, f32[2,2,512,128]{3,2,1,0:T(8,128)}, u32[]{:S(2)}, u32[]{:S(2)}) collective-permute-start(f32[2,2,512,128]{3,2,1,0:T(8,128)S(1)} %pad_maximum_fusion.refs_0_), channel_id=1, source_target_pairs={{0,64},{8,200},{64,128},{72,8},{128,192},{136,72},{192,0},{200,136... | collective-permute-start | bytes 3145736 | tf_op jit(solution)/shard_map/ppermute | solution.py:42
  45.6 16.3 %collective-permute-start.6 = (f32[512,512]{1,0:T(8,128)}, f32[512,512]{1,0:T(8,128)}, u32[]{:S(2)}, u32[]{:S(2)}) collective-permute-start(f32[512,512]{1,0:T(8,128)} %collective-permute-done.3.refs_5_.refs_7_.refs_9_), channel_id=1, source_target_pairs={{0,16},{8,60},{16,32},{24,8},{32,48},{40,24},{48,4},{56,40},{4,20}... | collective-permute-start | bytes 3145736 | tf_op jit(solution)/shard_map/ppermute | solution.py:32
  61.9 14.8 %collective-permute-start.9 = (f32[512,512]{1,0:T(8,128)S(1)}, f32[512,512]{1,0:T(8,128)S(1)}, u32[]{:S(2)}, u32[]{:S(2)}) collective-permute-start(f32[512,512]{1,0:T(8,128)S(1)} %copy-done.12), channel_id=1, source_target_pairs={{0,1},{8,11},{1,2},{9,8},{2,3},{10,9},{3,0},{11,10},{4,5},{12,15},... | collective-permute-start | bytes 3145736 | tf_op jit(solution)/shard_map/ppermute | solution.py:37
  62.0 16.2 %collective-permute-start.10 = (f32[512,512]{1,0:T(8,128)}, f32[512,512]{1,0:T(8,128)S(1)}, u32[]{:S(2)}, u32[]{:S(2)}) collective-permute-start(f32[512,512]{1,0:T(8,128)} %collective-permute-done.6.refs_6_.refs_8_.refs_10_), channel_id=1, source_target_pairs={{0,16},{8,60},{16,32},{24,8},{32,48},{40,24},{48,4},{56,40},{4,20}... | collective-permute-start | bytes 3145736 | tf_op jit(solution)/shard_map/ppermute | solution.py:32
  62.0 16.2 %collective-permute-start.13 = (f32[2,2,512,128]{3,2,1,0:T(8,128)}, f32[2,2,512,128]{3,2,1,0:T(8,128)}, u32[]{:S(2)}, u32[]{:S(2)}) collective-permute-start(f32[2,2,512,128]{3,2,1,0:T(8,128)} %collective-permute-done.7.refs_2_), channel_id=1, source_target_pairs={{0,64},{8,200},{64,128},{72,8},{128,192},{136,72},{192,0},{200,136... | collective-permute-start | bytes 3145736 | tf_op jit(solution)/shard_map/ppermute | solution.py:42
  63.2 25.2 %collective-permute-start.14 = (f32[2,2,512,128]{3,2,1,0:T(8,128)S(1)}, f32[2,2,512,128]{3,2,1,0:T(8,128)}, u32[]{:S(2)}, u32[]{:S(2)}) collective-permute-start(f32[2,2,512,128]{3,2,1,0:T(8,128)S(1)} %pad_maximum_fusion.1.refs_1_), channel_id=1, source_target_pairs={{0,64},{8,200},{64,128},{72,8},{128,192},{136,72},{192,0},{200,136... | collective-permute-start | bytes 3145736 | tf_op jit(solution)/shard_map/ppermute | solution.py:42
  76.7 16.0 %collective-permute-start.12 = (f32[512,512]{1,0:T(8,128)S(1)}, f32[512,512]{1,0:T(8,128)S(1)}, u32[]{:S(2)}, u32[]{:S(2)}) collective-permute-start(f32[512,512]{1,0:T(8,128)S(1)} %collective-permute-done.9.refs_2_), channel_id=1, source_target_pairs={{0,1},{8,11},{1,2},{9,8},{2,3},{10,9},{3,0},{11,10},{4,5},{12,15},... | collective-permute-start | bytes 3145736 | tf_op jit(solution)/shard_map/ppermute | solution.py:37
  78.2 16.0 %collective-permute-start.11 = (f32[512,512]{1,0:T(8,128)S(1)}, f32[512,512]{1,0:T(8,128)S(1)}, u32[]{:S(2)}, u32[]{:S(2)}) collective-permute-start(f32[512,512]{1,0:T(8,128)S(1)} %collective-permute-done.10.refs_7_.refs_9_.refs_11_), channel_id=1, source_target_pairs={{0,16},{8,60},{16,32},{24,8},{32,48},{40,24},{48,4},{56,40},{4,20}... | collective-permute-start | bytes 3145736 | tf_op jit(solution)/shard_map/ppermute | solution.py:32
  94.6 16.0 %collective-permute-start.15 = (f32[512,512]{1,0:T(8,128)S(1)}, f32[512,512]{1,0:T(8,128)}, u32[]{:S(2)}, u32[]{:S(2)}) collective-permute-start(f32[512,512]{1,0:T(8,128)S(1)} %shard_map.60.refs_4_), channel_id=1, source_target_pairs={{0,1},{8,11},{1,2},{9,8},{2,3},{10,9},{3,0},{11,10},{4,5},{12,15},... | collective-permute-start | bytes 3145736 | tf_op jit(solution)/shard_map/ppermute | solution.py:37
  97.3 16.1 %collective-permute-start.16 = (f32[512,512]{1,0:T(8,128)S(1)}, f32[512,512]{1,0:T(8,128)}, u32[]{:S(2)}, u32[]{:S(2)}) collective-permute-start(f32[512,512]{1,0:T(8,128)S(1)} %collective-permute-done.11.block.refs_8_.refs_10_.refs_12_), channel_id=1, source_target_pairs={{0,16},{8,60},{16,32},{24,8},{32,48},{40,24},{48,4},{56,40},{4,20}... | collective-permute-start | bytes 3145736 | tf_op jit(solution)/shard_map/ppermute | solution.py:32
  97.3 27.1 %collective-permute-start.19 = (f32[2,2,512,128]{3,2,1,0:T(8,128)}, f32[2,2,512,128]{3,2,1,0:T(8,128)}, u32[]{:S(2)}, u32[]{:S(2)}) collective-permute-start(f32[2,2,512,128]{3,2,1,0:T(8,128)} %collective-permute-done.13.refs_4_), channel_id=1, source_target_pairs={{0,64},{8,200},{64,128},{72,8},{128,192},{136,72},{192,0},{200,136... | collective-permute-start | bytes 3145736 | tf_op jit(solution)/shard_map/ppermute | solution.py:42
  98.5 25.9 %collective-permute-start.20 = (f32[2,2,512,128]{3,2,1,0:T(8,128)}, f32[2,2,512,128]{3,2,1,0:T(8,128)}, u32[]{:S(2)}, u32[]{:S(2)}) collective-permute-start(f32[2,2,512,128]{3,2,1,0:T(8,128)} %collective-permute-done.14.refs_3_), channel_id=1, source_target_pairs={{0,64},{8,200},{64,128},{72,8},{128,192},{136,72},{192,0},{200,136... | collective-permute-start | bytes 3145736 | tf_op jit(solution)/shard_map/ppermute | solution.py:42
  110.6 16.3 %collective-permute-start.18 = (f32[512,512]{1,0:T(8,128)}, f32[512,512]{1,0:T(8,128)}, u32[]{:S(2)}, u32[]{:S(2)}) collective-permute-start(f32[512,512]{1,0:T(8,128)} %collective-permute-done.15.refs_5_), channel_id=1, source_target_pairs={{0,1},{8,11},{1,2},{9,8},{2,3},{10,9},{3,0},{11,10},{4,5},{12,15},... | collective-permute-start | bytes 3145736 | tf_op jit(solution)/shard_map/ppermute | solution.py:37
  113.4 16.3 %collective-permute-start.17 = (f32[512,512]{1,0:T(8,128)}, f32[512,512]{1,0:T(8,128)}, u32[]{:S(2)}, u32[]{:S(2)}) collective-permute-start(f32[512,512]{1,0:T(8,128)} %collective-permute-done.16.refs_11_.refs_13_), channel_id=1, source_target_pairs={{0,16},{8,60},{16,32},{24,8},{32,48},{40,24},{48,4},{56,40},{4,20}... | collective-permute-start | bytes 3145736 | tf_op jit(solution)/shard_map/ppermute | solution.py:32
  129.8 15.0 %collective-permute-start.22 = (f32[512,512]{1,0:T(8,128)}, f32[512,512]{1,0:T(8,128)S(1)}, u32[]{:S(2)}, u32[]{:S(2)}) collective-permute-start(f32[512,512]{1,0:T(8,128)} %collective-permute-done.18.refs_6_), channel_id=1, source_target_pairs={{0,1},{8,11},{1,2},{9,8},{2,3},{10,9},{3,0},{11,10},{4,5},{12,15},... | collective-permute-start | bytes 3145736 | tf_op jit(solution)/shard_map/ppermute | solution.py:37
  131.9 15.0 %collective-permute-start.23 = (f32[2,2,512,128]{3,2,1,0:T(8,128)}, f32[2,2,512,128]{3,2,1,0:T(8,128)S(1)}, u32[]{:S(2)}, u32[]{:S(2)}) collective-permute-start(f32[2,2,512,128]{3,2,1,0:T(8,128)} %collective-permute-done.20.refs_5_), channel_id=1, source_target_pairs={{0,64},{8,200},{64,128},{72,8},{128,192},{136,72},{192,0},{200,136... | collective-permute-start | bytes 3145736 | tf_op jit(solution)/shard_map/ppermute | solution.py:42
  133.1 16.2 %collective-permute-start.21 = (f32[512,512]{1,0:T(8,128)}, f32[512,512]{1,0:T(8,128)S(1)}, u32[]{:S(2)}, u32[]{:S(2)}) collective-permute-start(f32[512,512]{1,0:T(8,128)} %collective-permute-done.17.refs_12_.refs_14_), channel_id=1, source_target_pairs={{0,16},{8,60},{16,32},{24,8},{32,48},{40,24},{48,4},{56,40},{4,20}... | collective-permute-start | bytes 3145736 | tf_op jit(solution)/shard_map/ppermute | solution.py:32
  163.7 13.6 %collective-permute-start.24 = (f32[2,512,512]{2,1,0:T(8,128)}, f32[2,512,512]{2,1,0:T(8,128)S(1)}, u32[]{:S(2)}, u32[]{:S(2)}) collective-permute-start(f32[2,512,512]{2,1,0:T(8,128)} %get-tuple-element.89), channel_id=1, source_target_pairs={{0,8},{8,0},{1,9},{9,1},{2,10},{10,2},{3,11},{11,3},{4,12},{12,4},... | collective-permute-start | bytes 6291464 | tf_op jit(solution)/shard_map/ppermute | solution.py:46
  189.3 16.7 %collective-permute-start.28 = (f32[256,512]{1,0:T(8,128)}, f32[256,512]{1,0:T(8,128)S(1)}, u32[]{:S(2)}, u32[]{:S(2)}) collective-permute-start(f32[256,512]{1,0:T(8,128)} %get-tuple-element.97), channel_id=1, source_target_pairs={{0,8},{8,0},{1,9},{9,1},{2,10},{10,2},{3,11},{11,3},{4,12},{12,4},... | collective-permute-start | bytes 1572872 | tf_op jit(solution)/shard_map/ppermute | solution.py:46
  193.2 12.9 %collective-permute-start.27 = (f32[256,512]{1,0:T(8,128)S(1)}, f32[256,512]{1,0:T(8,128)S(1)}, u32[]{:S(2)}, u32[]{:S(2)}) collective-permute-start(f32[256,512]{1,0:T(8,128)S(1)} %add.45), channel_id=1, source_target_pairs={{0,16},{8,60},{16,32},{24,8},{32,48},{40,24},{48,4},{56,40},{4,20}... | collective-permute-start | bytes 1572872 | tf_op jit(solution)/shard_map/ppermute | solution.py:32
  193.3 13.4 %collective-permute-start.34 = (f32[256,512]{1,0:T(8,128)S(1)}, f32[256,512]{1,0:T(8,128)S(1)}, u32[]{:S(2)}, u32[]{:S(2)}) collective-permute-start(f32[256,512]{1,0:T(8,128)S(1)} %copy-done.31), channel_id=1, source_target_pairs={{0,8},{8,0},{1,9},{9,1},{2,10},{10,2},{3,11},{11,3},{4,12},{12,4},... | collective-permute-start | bytes 1572872 | tf_op jit(solution)/shard_map/ppermute | solution.py:46
  193.9 15.4 %collective-permute-start.33 = (f32[256,512]{1,0:T(8,128)S(1)}, f32[256,512]{1,0:T(8,128)S(1)}, u32[]{:S(2)}, u32[]{:S(2)}) collective-permute-start(f32[256,512]{1,0:T(8,128)S(1)} %add.46), channel_id=1, source_target_pairs={{0,16},{8,60},{16,32},{24,8},{32,48},{40,24},{48,4},{56,40},{4,20}... | collective-permute-start | bytes 1572872 | tf_op jit(solution)/shard_map/ppermute | solution.py:32
  209.5 12.9 %collective-permute-start.35 = (f32[256,512]{1,0:T(8,128)S(1)}, f32[256,512]{1,0:T(8,128)S(1)}, u32[]{:S(2)}, u32[]{:S(2)}) collective-permute-start(f32[256,512]{1,0:T(8,128)S(1)} %add_add_fusion.2), channel_id=1, source_target_pairs={{0,16},{8,60},{16,32},{24,8},{32,48},{40,24},{48,4},{56,40},{4,20}... | collective-permute-start | bytes 1572872 | tf_op jit(solution)/shard_map/ppermute | solution.py:32
  209.6 14.8 %collective-permute-start.32 = (f32[256,512]{1,0:T(8,128)S(1)}, f32[256,512]{1,0:T(8,128)S(1)}, u32[]{:S(2)}, u32[]{:S(2)}) collective-permute-start(f32[256,512]{1,0:T(8,128)S(1)} %copy-done.30), channel_id=1, source_target_pairs={{0,8},{8,0},{1,9},{9,1},{2,10},{10,2},{3,11},{11,3},{4,12},{12,4},... | collective-permute-start | bytes 1572872 | tf_op jit(solution)/shard_map/ppermute | solution.py:46
  209.7 18.5 %collective-permute-start.38 = (f32[256,512]{1,0:T(8,128)S(1)}, f32[256,512]{1,0:T(8,128)S(1)}, u32[]{:S(2)}, u32[]{:S(2)}) collective-permute-start(f32[256,512]{1,0:T(8,128)S(1)} %copy-done.29), channel_id=1, source_target_pairs={{0,8},{8,0},{1,9},{9,1},{2,10},{10,2},{3,11},{11,3},{4,12},{12,4},... | collective-permute-start | bytes 1572872 | tf_op jit(solution)/shard_map/ppermute | solution.py:46
  216.9 11.1 %collective-permute-start.31 = (f32[256,512]{1,0:T(8,128)S(1)}, f32[256,512]{1,0:T(8,128)S(1)}, u32[]{:S(2)}, u32[]{:S(2)}) collective-permute-start(f32[256,512]{1,0:T(8,128)S(1)} %add_add_fusion.4), channel_id=1, source_target_pairs={{0,16},{8,60},{16,32},{24,8},{32,48},{40,24},{48,4},{56,40},{4,20}... | collective-permute-start | bytes 1572872 | tf_op jit(solution)/shard_map/ppermute | solution.py:32
  222.5 11.1 %collective-permute-start.37 = (f32[256,512]{1,0:T(8,128)S(1)}, f32[256,512]{1,0:T(8,128)S(1)}, u32[]{:S(2)}, u32[]{:S(2)}) collective-permute-start(f32[256,512]{1,0:T(8,128)S(1)} %add_add_fusion.1), channel_id=1, source_target_pairs={{0,16},{8,60},{16,32},{24,8},{32,48},{40,24},{48,4},{56,40},{4,20}... | collective-permute-start | bytes 1572872 | tf_op jit(solution)/shard_map/ppermute | solution.py:32
  (39 other events, 456.9 us)

commit v4 on v2

--- a/solution.py
+++ b/solution.py
@@ -17,6 +17,7 @@
 SMEM = pl.BlockSpec(memory_space=pltpu.SMEM)
 VMEM = pl.BlockSpec(memory_space=pltpu.VMEM)
 PARAMS = pltpu.CompilerParams(vmem_limit_bytes=56 << 20)
+MIDDLE = pltpu.CompilerParams(vmem_limit_bytes=40 << 20)
 SMALL = pltpu.CompilerParams(vmem_limit_bytes=16 << 20)
 
 
@@ -323,7 +324,7 @@
         in_specs=[SMEM] + [HBM] * (len(left) + 2),
         out_specs=(HBM,) + (VMEM,) * (4 * len(order)),
         scratch_shapes=[block, block, block, pair, pair],
-        compiler_params=PARAMS,
+        compiler_params=MIDDLE,
         cost_estimate=cost(2, n),
     )(place, *left, own, theirs)
 
@@ -346,7 +347,7 @@
         in_specs=[SMEM] + [HBM] * (len(left) + 1),
         out_specs=(VMEM,) * (4 * len(order)),
         scratch_shapes=[block, block, pltpu.SemaphoreType.DMA((2,)), pltpu.SemaphoreType.DMA],
-        compiler_params=PARAMS,
+        compiler_params=MIDDLE,
         cost_estimate=cost(dots, n),
     )(place, *left, right)
     return groups(outs, 4)

time: 226 us -> 222 us (0.982)
  Pallas kernels: 49.5 us -> 46 us
    unnamed x68 -> x50, local copies, waits for them, and re-layouts: 4.46 us -> 6.28 us
  transfers between devices with their start and end apart: 39 -> 39, of which waited for: 24 -> 25; matrix products, arithmetic and copies ran while one was open for 3% -> 2% of each run, Pallas kernels for 11% -> 10%
where the time goes in v4:
time: 222 us; the launch traced here: 221 us
  waiting for transfers between devices  119 us (54%)
  Pallas kernels  46 us (21%)
  starting transfers between devices  41.9 us (19%)
  local copies, waits for them, and re-layouts  6.96 us (3%)
  other arithmetic  6.58 us (3%)
    ppermute x7, waiting for transfers between devices, y_step(): return lax.ppermute(block, ('core', 'y'), pairs)  42.5 us
    pallas_call x2, Pallas kernels, accumulate(): pl.pallas_call(functools.partial(gather_kernel, have, had), out_shape=(sh...  27.9 us
    ppermute x13, waiting for transfers between devices, z_step(): return lax.ppermute(block, ('z_lo', 'core', 'z_hi'), pairs)  26.3 us
    ppermute x6, waiting for transfers between devices, x_step(): return lax.ppermute(block, ('leaf', 'core'), pairs)  21.6 us
    ppermute x2, waiting for transfers between devices, from_y(): return lax.ppermute(part, 'y', [(y, (y + k) % NY) for y in range(NY)])  14.6 us
    ppermute x11, waiting for transfers between devices, swap(): return lax.ppermute(block, axis, [(0, 1), (1, 0)])  14.1 us
    ppermute x11, starting transfers between devices, swap(): return lax.ppermute(block, axis, [(0, 1), (1, 0)])  13.9 us
    ppermute x13, starting transfers between devices, z_step(): return lax.ppermute(block, ('z_lo', 'core', 'z_hi'), pairs)  10.7 us
  transfers between devices with their start and end apart: 39, of which 25 were waited for; matrix products, arithmetic and copies ran while one was open for 2% of the time, Pallas kernels for 10%

profile of v4, /device:TPU:10, one launch (start us, length us, event | category | flops | bytes accessed | tf_op | source)
XLA Modules:
  0.0 221.5 jit_solution(958484191196378310)
XLA Ops:
  5.1 7.2 %collective-permute-start = (f32[512,128]{1,0:T(8,128)}, f32[512,128]{1,0:T(8,128)S(1)}, u32[]{:S(2)}, u32[]{:S(2)}) collective-permute-start(f32[512,128]{1,0:T(8,128)} %param.4), channel_id=1, source_target_pairs={{0,4},{4,0},{1,5},{5,1},{2,6},{6,2},{3,7},{7,3},{8,12},{12,8},{9,1... | collective-permute-start | bytes 786440 | tf_op jit(solution)/shard_map/ppermute | solution.py:47
  12.3 6.2 %collective-permute-done = f32[512,128]{1,0:T(8,128)S(1)} collective-permute-done((f32[512,128]{1,0:T(8,128)}, f32[512,128]{1,0:T(8,128)S(1)}, u32[]{:S(2)}, u32[]{:S(2)}) %collective-permute-start) | collective-permute-done | bytes 262176 | tf_op jit(solution)/shard_map/ppermute | solution.py:47
  21.2 5.7 %collective-permute-start.3 = (f32[512,512]{1,0:T(8,128)S(1)}, f32[512,512]{1,0:T(8,128)}, u32[]{:S(2)}, u32[]{:S(2)}) collective-permute-start(f32[512,512]{1,0:T(8,128)S(1)} %get-tuple-element.54.refs_6_.refs_8_), channel_id=1, source_target_pairs={{0,16},{8,60},{16,32},{24,8},{32,48},{40,24},{48,4},{56,40},{4,20}... | collective-permute-start | bytes 3145736 | tf_op jit(solution)/shard_map/ppermute | solution.py:33
  26.9 2.4 %collective-permute-start.5 = (f32[2,512,128]{2,1,0:T(8,128)S(1)}, f32[2,512,128]{2,1,0:T(8,128)}, u32[]{:S(2)}, u32[]{:S(2)}) collective-permute-start(f32[2,512,128]{2,1,0:T(8,128)S(1)} %pad_maximum_fusion.2), channel_id=1, source_target_pairs={{0,3},{1,0},{2,1},{3,2},{4,7},{5,4},{6,5},{7,6},{8,11},{9,8},{10,9... | collective-permute-start | bytes 1572872 | tf_op jit(solution)/shard_map/ppermute | solution.py:382
  29.3 12.2 %collective-permute-done.5 = f32[2,512,128]{2,1,0:T(8,128)} collective-permute-done((f32[2,512,128]{2,1,0:T(8,128)S(1)}, f32[2,512,128]{2,1,0:T(8,128)}, u32[]{:S(2)}, u32[]{:S(2)}) %collective-permute-start.5) | collective-permute-done | bytes 524320 | tf_op jit(solution)/shard_map/ppermute | solution.py:382
  41.5 2.4 %collective-permute-done.4 = f32[2,512,128]{2,1,0:T(8,128)S(1)} collective-permute-done((f32[2,512,128]{2,1,0:T(8,128)S(1)}, f32[2,512,128]{2,1,0:T(8,128)S(1)}, u32[]{:S(2)}, u32[]{:S(2)}) %collective-permute-start.4) | collective-permute-done | bytes 524320 | tf_op jit(solution)/shard_map/ppermute | solution.py:382
  47.8 9.1 %collective-permute-done.8 = f32[2,512,128]{2,1,0:T(8,128)S(1)} collective-permute-done((f32[2,512,128]{2,1,0:T(8,128)S(1)}, f32[2,512,128]{2,1,0:T(8,128)S(1)}, u32[]{:S(2)}, u32[]{:S(2)}) %collective-permute-start.8) | collective-permute-done | bytes 524320 | tf_op jit(solution)/shard_map/ppermute | solution.py:38
  58.0 2.1 collective-permute-done.7.refs_2_
  60.1 2.6 %collective-permute-done.6.refs_8_.refs_10_ = f32[512,512]{1,0:T(8,128)S(1)} collective-permute-done((f32[512,512]{1,0:T(8,128)}, f32[512,512]{1,0:T(8,128)S(1)}, u32[]{:S(2)}, u32[]{:S(2)}) %collective-permute-start.6) | collective-permute-done | bytes 1048608 | tf_op jit(solution)/shard_map/ppermute | solution.py:33
  64.6 12.9 %collective-permute-done.9.refs_2_ = f32[512,512]{1,0:T(8,128)S(1)} collective-permute-done((f32[512,512]{1,0:T(8,128)S(1)}, f32[512,512]{1,0:T(8,128)S(1)}, u32[]{:S(2)}, u32[]{:S(2)}) %collective-permute-start.9) | collective-permute-done | bytes 1048608 | tf_op jit(solution)/shard_map/ppermute | solution.py:38
  78.9 10.3 %collective-permute-done.14.refs_3_ = f32[2,2,512,128]{3,2,1,0:T(8,128)S(1)} collective-permute-done((f32[2,2,512,128]{3,2,1,0:T(8,128)S(1)}, f32[2,2,512,128]{3,2,1,0:T(8,128)S(1)}, u32[]{:S(2)}, u32[]{:S(2)}) %collective-permute-start.14) | collective-permute-done | bytes 1048608 | tf_op jit(solution)/shard_map/ppermute | solution.py:43
  89.2 4.3 %collective-permute-done.12.refs_3_ = f32[512,512]{1,0:T(8,128)S(1)} collective-permute-done((f32[512,512]{1,0:T(8,128)S(1)}, f32[512,512]{1,0:T(8,128)S(1)}, u32[]{:S(2)}, u32[]{:S(2)}) %collective-permute-start.12) | collective-permute-done | bytes 1048608 | tf_op jit(solution)/shard_map/ppermute | solution.py:38
  95.2 2.1 collective-permute-start.15
  98.9 12.2 %collective-permute-done.15.refs_5_ = f32[512,512]{1,0:T(8,128)S(1)} collective-permute-done((f32[512,512]{1,0:T(8,128)S(1)}, f32[512,512]{1,0:T(8,128)S(1)}, u32[]{:S(2)}, u32[]{:S(2)}) %collective-permute-start.15) | collective-permute-done | bytes 1048608 | tf_op jit(solution)/shard_map/ppermute | solution.py:38
  111.1 2.1 collective-permute-start.18
  114.3 9.1 %collective-permute-done.20.refs_5_ = f32[2,2,512,128]{3,2,1,0:T(8,128)} collective-permute-done((f32[2,2,512,128]{3,2,1,0:T(8,128)S(1)}, f32[2,2,512,128]{3,2,1,0:T(8,128)}, u32[]{:S(2)}, u32[]{:S(2)}) %collective-permute-start.20) | collective-permute-done | bytes 1048608 | tf_op jit(solution)/shard_map/ppermute | solution.py:43
  123.4 3.8 %collective-permute-done.18.refs_6_ = f32[512,512]{1,0:T(8,128)} collective-permute-done((f32[512,512]{1,0:T(8,128)S(1)}, f32[512,512]{1,0:T(8,128)}, u32[]{:S(2)}, u32[]{:S(2)}) %collective-permute-start.18) | collective-permute-done | bytes 1048608 | tf_op jit(solution)/shard_map/ppermute | solution.py:38
  127.3 3.1 %collective-permute-done.17.refs_12_.refs_14_ = f32[512,512]{1,0:T(8,128)} collective-permute-done((f32[512,512]{1,0:T(8,128)S(1)}, f32[512,512]{1,0:T(8,128)}, u32[]{:S(2)}, u32[]{:S(2)}) %collective-permute-start.17) | collective-permute-done | bytes 1048608 | tf_op jit(solution)/shard_map/ppermute | solution.py:33
  130.4 2.7 %collective-permute-start.22 = (f32[512,512]{1,0:T(8,128)}, f32[512,512]{1,0:T(8,128)}, u32[]{:S(2)}, u32[]{:S(2)}) collective-permute-start(f32[512,512]{1,0:T(8,128)} %collective-permute-done.18.refs_6_), channel_id=1, source_target_pairs={{0,1},{8,11},{1,2},{9,8},{2,3},{10,9},{3,0},{11,10},{4,5},{12,15},... | collective-permute-start | bytes 3145736 | tf_op jit(solution)/shard_map/ppermute | solution.py:38
  135.0 14.0 %shard_map.61 = (f32[2,512,512]{2,1,0:T(8,128)}, f32[2,512,512]{2,1,0:T(8,128)}) custom-call(s32[5]{0:T(128)} %stack.50.place, f32[2,2,512,128]{3,2,1,0:T(8,128)} %pad_maximum_fusion.refs_0_, f32[2,2,512,128]{3,2,1,0:T(8,128)} %copy-done.15, f32[2,2,512,128]{3,2,1,0:T(8,128)} %collective-permute-done.7.refs_2_, f32[2,2,512,128]{3,2,1,0:T(8,128)} %copy-done.22, ...), custom_call_target="tpu_custom_call" | custom-call | flops 4831838208 | bytes 18874368 | tf_op jit(solution)/shard_map/pallas_call | solution.py:283
  150.6 13.9 %shard_map.62 = (f32[2,512,512]{2,1,0:T(8,128)}, f32[2,512,512]{2,1,0:T(8,128)}) custom-call(s32[5]{0:T(128)} %stack.50.place, f32[2,2,512,128]{3,2,1,0:T(8,128)} %pad_maximum_fusion.refs_0_, f32[2,2,512,128]{3,2,1,0:T(8,128)} %copy-done.15, f32[2,2,512,128]{3,2,1,0:T(8,128)} %collective-permute-done.7.refs_2_, ...), custom_call_target="tpu_custom_call", output_to_operand_aliasing={{0}: (17, {}), {1}: (18, {})} | custom-call | flops 4831838208 | bytes 18874368 | tf_op jit(solution)/shard_map/pallas_call | solution.py:283
  164.7 4.4 %collective-permute-done.24.refs_9_ = f32[2,512,512]{2,1,0:T(8,128)S(1)} collective-permute-done((f32[2,512,512]{2,1,0:T(8,128)}, f32[2,512,512]{2,1,0:T(8,128)S(1)}, u32[]{:S(2)}, u32[]{:S(2)}) %collective-permute-start.24) | collective-permute-done | bytes 2097184 | tf_op jit(solution)/shard_map/ppermute | solution.py:47
  170.4 8.1 %shard_map.63 = (f32[2,512,512]{2,1,0:T(8,128)}, f32[256,512]{1,0:T(8,128)S(1)}, f32[256,512]{1,0:T(8,128)S(1)}, f32[256,512]{1,0:T(8,128)S(1)}, f32[256,512]{1,...) custom-call(s32[5]{0:T(128)S(1)} %copy-done.12, ...), custom_call_target="tpu_custom_call" | custom-call | flops 1610612736 | bytes 6291456 | tf_op jit(solution)/shard_map/pallas_call | solution.py:321
  181.6 3.0 %collective-permute-start.34 = (f32[256,512]{1,0:T(8,128)S(1)}, f32[256,512]{1,0:T(8,128)S(1)}, u32[]{:S(2)}, u32[]{:S(2)}) collective-permute-start(f32[256,512]{1,0:T(8,128)S(1)} %get-tuple-element.97), channel_id=1, source_target_pairs={{0,8},{8,0},{1,9},{9,1},{2,10},{10,2},{3,11},{11,3},{4,12},{12,4},... | collective-permute-start | bytes 1572872 | tf_op jit(solution)/shard_map/ppermute | solution.py:47
  184.6 7.1 %shard_map.65 = (f32[256,512]{1,0:T(8,128)S(1)}, f32[256,512]{1,0:T(8,128)S(1)}, f32[256,512]{1,0:T(8,128)S(1)}, f32[256,512]{1,0:T(8,128)S(1)}, f32[256,512]{1,...) custom-call(s32[5]{0:T(128)S(1)} %copy-done.12, ...), custom_call_target="tpu_custom_call" | custom-call | tf_op jit(solution)/shard_map/pallas_call | solution.py:344
  192.7 2.5 %collective-permute-start.29 = (f32[256,512]{1,0:T(8,128)S(1)}, f32[256,512]{1,0:T(8,128)S(1)}, u32[]{:S(2)}, u32[]{:S(2)}) collective-permute-start(f32[256,512]{1,0:T(8,128)S(1)} %add_add_fusion.5), channel_id=1, source_target_pairs={{0,16},{8,60},{16,32},{24,8},{32,48},{40,24},{48,4},{56,40},{4,20}... | collective-permute-start | bytes 1572872 | tf_op jit(solution)/shard_map/ppermute | solution.py:33
  195.2 2.5 %collective-permute-done.33 = f32[256,512]{1,0:T(8,128)S(1)} collective-permute-done((f32[256,512]{1,0:T(8,128)S(1)}, f32[256,512]{1,0:T(8,128)S(1)}, u32[]{:S(2)}, u32[]{:S(2)}) %collective-permute-start.33) | collective-permute-done | bytes 524320 | tf_op jit(solution)/shard_map/ppermute | solution.py:33
  197.9 1.9 collective-permute-start.32
  199.7 3.5 %collective-permute-done.29 = f32[256,512]{1,0:T(8,128)S(1)} collective-permute-done((f32[256,512]{1,0:T(8,128)S(1)}, f32[256,512]{1,0:T(8,128)S(1)}, u32[]{:S(2)}, u32[]{:S(2)}) %collective-permute-start.29) | collective-permute-done | bytes 524320 | tf_op jit(solution)/shard_map/ppermute | solution.py:33
  204.6 4.3 %collective-permute-done.35 = f32[256,512]{1,0:T(8,128)S(1)} collective-permute-done((f32[256,512]{1,0:T(8,128)S(1)}, f32[256,512]{1,0:T(8,128)S(1)}, u32[]{:S(2)}, u32[]{:S(2)}) %collective-permute-start.35) | collective-permute-done | bytes 524320 | tf_op jit(solution)/shard_map/ppermute | solution.py:33
  211.9 2.6 %collective-permute-done.31 = f32[256,512]{1,0:T(8,128)S(1)} collective-permute-done((f32[256,512]{1,0:T(8,128)S(1)}, f32[256,512]{1,0:T(8,128)S(1)}, u32[]{:S(2)}, u32[]{:S(2)}) %collective-permute-start.31) | collective-permute-done | bytes 524320 | tf_op jit(solution)/shard_map/ppermute | solution.py:33
  214.6 5.5 %collective-permute-done.37 = f32[256,512]{1,0:T(8,128)S(1)} collective-permute-done((f32[256,512]{1,0:T(8,128)S(1)}, f32[256,512]{1,0:T(8,128)S(1)}, u32[]{:S(2)}, u32[]{:S(2)}) %collective-permute-start.37) | collective-permute-done | bytes 524320 | tf_op jit(solution)/shard_map/ppermute | solution.py:33
  (118 shorter events, 34.6 us)
Async XLA Ops:
  3.4 17.7 %collective-permute-start.2 = (f32[512,512]{1,0:T(8,128)S(1)}, f32[512,512]{1,0:T(8,128)S(1)}, u32[]{:S(2)}, u32[]{:S(2)}) collective-permute-start(f32[512,512]{1,0:T(8,128)S(1)} %get-tuple-element.52.refs_0_), channel_id=1, source_target_pairs={{0,1},{8,11},{1,2},{9,8},{2,3},{10,9},{3,0},{11,10},{4,5},{12,15},... | collective-permute-start | bytes 3145736 | tf_op jit(solution)/shard_map/ppermute | solution.py:38
  5.1 13.4 %collective-permute-start = (f32[512,128]{1,0:T(8,128)}, f32[512,128]{1,0:T(8,128)S(1)}, u32[]{:S(2)}, u32[]{:S(2)}) collective-permute-start(f32[512,128]{1,0:T(8,128)} %param.4), channel_id=1, source_target_pairs={{0,4},{4,0},{1,5},{5,1},{2,6},{6,2},{3,7},{7,3},{8,12},{12,8},{9,1... | collective-permute-start | bytes 786440 | tf_op jit(solution)/shard_map/ppermute | solution.py:47
  21.2 22.7 %collective-permute-start.3 = (f32[512,512]{1,0:T(8,128)S(1)}, f32[512,512]{1,0:T(8,128)}, u32[]{:S(2)}, u32[]{:S(2)}) collective-permute-start(f32[512,512]{1,0:T(8,128)S(1)} %get-tuple-element.54.refs_6_.refs_8_), channel_id=1, source_target_pairs={{0,16},{8,60},{16,32},{24,8},{32,48},{40,24},{48,4},{56,40},{4,20}... | collective-permute-start | bytes 3145736 | tf_op jit(solution)/shard_map/ppermute | solution.py:33
  26.9 14.6 %collective-permute-start.5 = (f32[2,512,128]{2,1,0:T(8,128)S(1)}, f32[2,512,128]{2,1,0:T(8,128)}, u32[]{:S(2)}, u32[]{:S(2)}) collective-permute-start(f32[2,512,128]{2,1,0:T(8,128)S(1)} %pad_maximum_fusion.2), channel_id=1, source_target_pairs={{0,3},{1,0},{2,1},{3,2},{4,7},{5,4},{6,5},{7,6},{8,11},{9,8},{10,9... | collective-permute-start | bytes 1572872 | tf_op jit(solution)/shard_map/ppermute | solution.py:382
  29.3 14.6 %collective-permute-start.4 = (f32[2,512,128]{2,1,0:T(8,128)S(1)}, f32[2,512,128]{2,1,0:T(8,128)S(1)}, u32[]{:S(2)}, u32[]{:S(2)}) collective-permute-start(f32[2,512,128]{2,1,0:T(8,128)S(1)} %pad_maximum_fusion.2), channel_id=1, source_target_pairs={{0,1},{1,2},{2,3},{3,0},{4,5},{5,6},{6,7},{7,4},{8,9},{9,10},{10,1... | collective-permute-start | bytes 1572872 | tf_op jit(solution)/shard_map/ppermute | solution.py:382
  45.0 15.1 %collective-permute-start.7 = (f32[2,2,512,128]{3,2,1,0:T(8,128)}, f32[2,2,512,128]{3,2,1,0:T(8,128)}, u32[]{:S(2)}, u32[]{:S(2)}) collective-permute-start(f32[2,2,512,128]{3,2,1,0:T(8,128)} %pad_maximum_fusion.refs_0_), channel_id=1, source_target_pairs={{0,64},{8,200},{64,128},{72,8},{128,192},{136,72},{192,0},{200,136... | collective-permute-start | bytes 3145736 | tf_op jit(solution)/shard_map/ppermute | solution.py:43
  46.5 16.2 %collective-permute-start.6 = (f32[512,512]{1,0:T(8,128)}, f32[512,512]{1,0:T(8,128)S(1)}, u32[]{:S(2)}, u32[]{:S(2)}) collective-permute-start(f32[512,512]{1,0:T(8,128)} %collective-permute-done.3.refs_7_.refs_9_), channel_id=1, source_target_pairs={{0,16},{8,60},{16,32},{24,8},{32,48},{40,24},{48,4},{56,40},{4,20}... | collective-permute-start | bytes 3145736 | tf_op jit(solution)/shard_map/ppermute | solution.py:33
  62.7 14.8 %collective-permute-start.9 = (f32[512,512]{1,0:T(8,128)S(1)}, f32[512,512]{1,0:T(8,128)S(1)}, u32[]{:S(2)}, u32[]{:S(2)}) collective-permute-start(f32[512,512]{1,0:T(8,128)S(1)} %collective-permute-done.2.refs_1_), channel_id=1, source_target_pairs={{0,1},{8,11},{1,2},{9,8},{2,3},{10,9},{3,0},{11,10},{4,5},{12,15},... | collective-permute-start | bytes 3145736 | tf_op jit(solution)/shard_map/ppermute | solution.py:38
  62.8 16.0 %collective-permute-start.10 = (f32[512,512]{1,0:T(8,128)S(1)}, f32[512,512]{1,0:T(8,128)S(1)}, u32[]{:S(2)}, u32[]{:S(2)}) collective-permute-start(f32[512,512]{1,0:T(8,128)S(1)} %collective-permute-done.6.refs_8_.refs_10_), channel_id=1, source_target_pairs={{0,16},{8,60},{16,32},{24,8},{32,48},{40,24},{48,4},{56,40},{4,20}... | collective-permute-start | bytes 3145736 | tf_op jit(solution)/shard_map/ppermute | solution.py:33
  62.8 16.0 %collective-permute-start.13 = (f32[2,2,512,128]{3,2,1,0:T(8,128)}, f32[2,2,512,128]{3,2,1,0:T(8,128)S(1)}, u32[]{:S(2)}, u32[]{:S(2)}) collective-permute-start(f32[2,2,512,128]{3,2,1,0:T(8,128)} %collective-permute-done.7.refs_2_), channel_id=1, source_target_pairs={{0,64},{8,200},{64,128},{72,8},{128,192},{136,72},{192,0},{200,136... | collective-permute-start | bytes 3145736 | tf_op jit(solution)/shard_map/ppermute | solution.py:43
  64.1 25.0 %collective-permute-start.14 = (f32[2,2,512,128]{3,2,1,0:T(8,128)S(1)}, f32[2,2,512,128]{3,2,1,0:T(8,128)S(1)}, u32[]{:S(2)}, u32[]{:S(2)}) collective-permute-start(f32[2,2,512,128]{3,2,1,0:T(8,128)S(1)} %pad_maximum_fusion.1.refs_1_), channel_id=1, source_target_pairs={{0,64},{8,200},{64,128},{72,8},{128,192},{136,72},{192,0},{200,136... | collective-permute-start | bytes 3145736 | tf_op jit(solution)/shard_map/ppermute | solution.py:43
  77.5 16.0 %collective-permute-start.12 = (f32[512,512]{1,0:T(8,128)S(1)}, f32[512,512]{1,0:T(8,128)S(1)}, u32[]{:S(2)}, u32[]{:S(2)}) collective-permute-start(f32[512,512]{1,0:T(8,128)S(1)} %collective-permute-done.9.refs_2_), channel_id=1, source_target_pairs={{0,1},{8,11},{1,2},{9,8},{2,3},{10,9},{3,0},{11,10},{4,5},{12,15},... | collective-permute-start | bytes 3145736 | tf_op jit(solution)/shard_map/ppermute | solution.py:38
  78.8 16.0 %collective-permute-start.11 = (f32[512,512]{1,0:T(8,128)S(1)}, f32[512,512]{1,0:T(8,128)S(1)}, u32[]{:S(2)}, u32[]{:S(2)}) collective-permute-start(f32[512,512]{1,0:T(8,128)S(1)} %collective-permute-done.10.refs_9_.refs_11_), channel_id=1, source_target_pairs={{0,16},{8,60},{16,32},{24,8},{32,48},{40,24},{48,4},{56,40},{4,20}... | collective-permute-start | bytes 3145736 | tf_op jit(solution)/shard_map/ppermute | solution.py:33
  95.2 15.9 %collective-permute-start.15 = (f32[512,512]{1,0:T(8,128)S(1)}, f32[512,512]{1,0:T(8,128)S(1)}, u32[]{:S(2)}, u32[]{:S(2)}) collective-permute-start(f32[512,512]{1,0:T(8,128)S(1)} %shard_map.60.refs_4_), channel_id=1, source_target_pairs={{0,1},{8,11},{1,2},{9,8},{2,3},{10,9},{3,0},{11,10},{4,5},{12,15},... | collective-permute-start | bytes 3145736 | tf_op jit(solution)/shard_map/ppermute | solution.py:38
  97.3 17.0 %collective-permute-start.16 = (f32[512,512]{1,0:T(8,128)S(1)}, f32[512,512]{1,0:T(8,128)S(1)}, u32[]{:S(2)}, u32[]{:S(2)}) collective-permute-start(f32[512,512]{1,0:T(8,128)S(1)} %collective-permute-done.11.block.refs_10_.refs_12_), channel_id=1, source_target_pairs={{0,16},{8,60},{16,32},{24,8},{32,48},{40,24},{48,4},{56,40},{4,20}... | collective-permute-start | bytes 3145736 | tf_op jit(solution)/shard_map/ppermute | solution.py:33
  97.3 17.0 %collective-permute-start.19 = (f32[2,2,512,128]{3,2,1,0:T(8,128)S(1)}, f32[2,2,512,128]{3,2,1,0:T(8,128)S(1)}, u32[]{:S(2)}, u32[]{:S(2)}) collective-permute-start(f32[2,2,512,128]{3,2,1,0:T(8,128)S(1)} %collective-permute-done.13.refs_4_), channel_id=1, source_target_pairs={{0,64},{8,200},{64,128},{72,8},{128,192},{136,72},{192,0},{200,136... | collective-permute-start | bytes 3145736 | tf_op jit(solution)/shard_map/ppermute | solution.py:43
  98.5 24.9 %collective-permute-start.20 = (f32[2,2,512,128]{3,2,1,0:T(8,128)S(1)}, f32[2,2,512,128]{3,2,1,0:T(8,128)}, u32[]{:S(2)}, u32[]{:S(2)}) collective-permute-start(f32[2,2,512,128]{3,2,1,0:T(8,128)S(1)} %collective-permute-done.14.refs_3_), channel_id=1, source_target_pairs={{0,64},{8,200},{64,128},{72,8},{128,192},{136,72},{192,0},{200,136... | collective-permute-start | bytes 3145736 | tf_op jit(solution)/shard_map/ppermute | solution.py:43
  111.1 16.1 %collective-permute-start.18 = (f32[512,512]{1,0:T(8,128)S(1)}, f32[512,512]{1,0:T(8,128)}, u32[]{:S(2)}, u32[]{:S(2)}) collective-permute-start(f32[512,512]{1,0:T(8,128)S(1)} %collective-permute-done.15.refs_5_), channel_id=1, source_target_pairs={{0,1},{8,11},{1,2},{9,8},{2,3},{10,9},{3,0},{11,10},{4,5},{12,15},... | collective-permute-start | bytes 3145736 | tf_op jit(solution)/shard_map/ppermute | solution.py:38
  114.3 16.1 %collective-permute-start.17 = (f32[512,512]{1,0:T(8,128)S(1)}, f32[512,512]{1,0:T(8,128)}, u32[]{:S(2)}, u32[]{:S(2)}) collective-permute-start(f32[512,512]{1,0:T(8,128)S(1)} %collective-permute-done.16.refs_11_.refs_13_), channel_id=1, source_target_pairs={{0,16},{8,60},{16,32},{24,8},{32,48},{40,24},{48,4},{56,40},{4,20}... | collective-permute-start | bytes 3145736 | tf_op jit(solution)/shard_map/ppermute | solution.py:33
  130.4 18.6 %collective-permute-start.22 = (f32[512,512]{1,0:T(8,128)}, f32[512,512]{1,0:T(8,128)}, u32[]{:S(2)}, u32[]{:S(2)}) collective-permute-start(f32[512,512]{1,0:T(8,128)} %collective-permute-done.18.refs_6_), channel_id=1, source_target_pairs={{0,1},{8,11},{1,2},{9,8},{2,3},{10,9},{3,0},{11,10},{4,5},{12,15},... | collective-permute-start | bytes 3145736 | tf_op jit(solution)/shard_map/ppermute | solution.py:38
  133.1 15.9 %collective-permute-start.23 = (f32[2,2,512,128]{3,2,1,0:T(8,128)}, f32[2,2,512,128]{3,2,1,0:T(8,128)}, u32[]{:S(2)}, u32[]{:S(2)}) collective-permute-start(f32[2,2,512,128]{3,2,1,0:T(8,128)} %collective-permute-done.20.refs_5_), channel_id=1, source_target_pairs={{0,64},{8,200},{64,128},{72,8},{128,192},{136,72},{192,0},{200,136... | collective-permute-start | bytes 3145736 | tf_op jit(solution)/shard_map/ppermute | solution.py:43
  134.3 16.3 %collective-permute-start.21 = (f32[512,512]{1,0:T(8,128)}, f32[512,512]{1,0:T(8,128)}, u32[]{:S(2)}, u32[]{:S(2)}) collective-permute-start(f32[512,512]{1,0:T(8,128)} %collective-permute-done.17.refs_12_.refs_14_), channel_id=1, source_target_pairs={{0,16},{8,60},{16,32},{24,8},{32,48},{40,24},{48,4},{56,40},{4,20}... | collective-permute-start | bytes 3145736 | tf_op jit(solution)/shard_map/ppermute | solution.py:33
  179.3 13.1 %collective-permute-start.28 = (f32[256,512]{1,0:T(8,128)S(1)}, f32[256,512]{1,0:T(8,128)S(1)}, u32[]{:S(2)}, u32[]{:S(2)}) collective-permute-start(f32[256,512]{1,0:T(8,128)S(1)} %get-tuple-element.89), channel_id=1, source_target_pairs={{0,8},{8,0},{1,9},{9,1},{2,10},{10,2},{3,11},{11,3},{4,12},{12,4},... | collective-permute-start | bytes 1572872 | tf_op jit(solution)/shard_map/ppermute | solution.py:47
  181.5 11.0 %collective-permute-start.27 = (f32[256,512]{1,0:T(8,128)S(1)}, f32[256,512]{1,0:T(8,128)S(1)}, u32[]{:S(2)}, u32[]{:S(2)}) collective-permute-start(f32[256,512]{1,0:T(8,128)S(1)} %add.45), channel_id=1, source_target_pairs={{0,16},{8,60},{16,32},{24,8},{32,48},{40,24},{48,4},{56,40},{4,20}... | collective-permute-start | bytes 1572872 | tf_op jit(solution)/shard_map/ppermute | solution.py:33
  181.6 13.5 %collective-permute-start.34 = (f32[256,512]{1,0:T(8,128)S(1)}, f32[256,512]{1,0:T(8,128)S(1)}, u32[]{:S(2)}, u32[]{:S(2)}) collective-permute-start(f32[256,512]{1,0:T(8,128)S(1)} %get-tuple-element.97), channel_id=1, source_target_pairs={{0,8},{8,0},{1,9},{9,1},{2,10},{10,2},{3,11},{11,3},{4,12},{12,4},... | collective-permute-start | bytes 1572872 | tf_op jit(solution)/shard_map/ppermute | solution.py:47
  184.6 13.0 %collective-permute-start.33 = (f32[256,512]{1,0:T(8,128)S(1)}, f32[256,512]{1,0:T(8,128)S(1)}, u32[]{:S(2)}, u32[]{:S(2)}) collective-permute-start(f32[256,512]{1,0:T(8,128)S(1)} %add.46), channel_id=1, source_target_pairs={{0,16},{8,60},{16,32},{24,8},{32,48},{40,24},{48,4},{56,40},{4,20}... | collective-permute-start | bytes 1572872 | tf_op jit(solution)/shard_map/ppermute | solution.py:33
  192.4 12.2 %collective-permute-start.36 = (f32[256,512]{1,0:T(8,128)S(1)}, f32[256,512]{1,0:T(8,128)S(1)}, u32[]{:S(2)}, u32[]{:S(2)}) collective-permute-start(f32[256,512]{1,0:T(8,128)S(1)} %get-tuple-element.99), channel_id=1, source_target_pairs={{0,8},{8,0},{1,9},{9,1},{2,10},{10,2},{3,11},{11,3},{4,12},{12,4},... | collective-permute-start | bytes 1572872 | tf_op jit(solution)/shard_map/ppermute | solution.py:47
  197.8 11.1 %collective-permute-start.35 = (f32[256,512]{1,0:T(8,128)S(1)}, f32[256,512]{1,0:T(8,128)S(1)}, u32[]{:S(2)}, u32[]{:S(2)}) collective-permute-start(f32[256,512]{1,0:T(8,128)S(1)} %add_add_fusion.2), channel_id=1, source_target_pairs={{0,16},{8,60},{16,32},{24,8},{32,48},{40,24},{48,4},{56,40},{4,20}... | collective-permute-start | bytes 1572872 | tf_op jit(solution)/shard_map/ppermute | solution.py:33
  197.9 14.0 %collective-permute-start.32 = (f32[256,512]{1,0:T(8,128)S(1)}, f32[256,512]{1,0:T(8,128)S(1)}, u32[]{:S(2)}, u32[]{:S(2)}) collective-permute-start(f32[256,512]{1,0:T(8,128)S(1)} %get-tuple-element.94), channel_id=1, source_target_pairs={{0,8},{8,0},{1,9},{9,1},{2,10},{10,2},{3,11},{11,3},{4,12},{12,4},... | collective-permute-start | bytes 1572872 | tf_op jit(solution)/shard_map/ppermute | solution.py:47
  199.7 14.9 %collective-permute-start.38 = (f32[256,512]{1,0:T(8,128)S(1)}, f32[256,512]{1,0:T(8,128)S(1)}, u32[]{:S(2)}, u32[]{:S(2)}) collective-permute-start(f32[256,512]{1,0:T(8,128)S(1)} %get-tuple-element.101), channel_id=1, source_target_pairs={{0,8},{8,0},{1,9},{9,1},{2,10},{10,2},{3,11},{11,3},{4,12},{12,4},... | collective-permute-start | bytes 1572872 | tf_op jit(solution)/shard_map/ppermute | solution.py:47
  203.4 11.1 %collective-permute-start.31 = (f32[256,512]{1,0:T(8,128)S(1)}, f32[256,512]{1,0:T(8,128)S(1)}, u32[]{:S(2)}, u32[]{:S(2)}) collective-permute-start(f32[256,512]{1,0:T(8,128)S(1)} %add_add_fusion.4), channel_id=1, source_target_pairs={{0,16},{8,60},{16,32},{24,8},{32,48},{40,24},{48,4},{56,40},{4,20}... | collective-permute-start | bytes 1572872 | tf_op jit(solution)/shard_map/ppermute | solution.py:33
  209.0 11.1 %collective-permute-start.37 = (f32[256,512]{1,0:T(8,128)S(1)}, f32[256,512]{1,0:T(8,128)S(1)}, u32[]{:S(2)}, u32[]{:S(2)}) collective-permute-start(f32[256,512]{1,0:T(8,128)S(1)} %add_add_fusion.1), channel_id=1, source_target_pairs={{0,16},{8,60},{16,32},{24,8},{32,48},{40,24},{48,4},{56,40},{4,20}... | collective-permute-start | bytes 1572872 | tf_op jit(solution)/shard_map/ppermute | solution.py:33
  (32 other events, 482.8 us)
